TPU v7x, 32 devices: a whole 2x2x4 slice. The times are simulated.
32 devices in a mesh: groups: 2 (over y), ops: 16 (over z, x, core).
Axes of the slice: x: 2, y: 2, z: 4, core: 2. Of those that a mesh axis runs over, the one named last changes fastest.
Arguments:
- normal_ops: bfloat16 [256, 640, 640], P(('groups', 'ops')), parts along dimension 0, may hold values from -6 to 6
- rotation_one: bfloat16 [5120, 640], P(('groups', 'ops')), parts along dimension 0, may hold values from -0.25 to 0.25
- rotation_two: bfloat16 [5120, 640], P(('groups', 'ops')), parts along dimension 0, may hold values from -0.25 to 0.25
- integrals: float32 [64, 32], P('groups'), parts along dimension 0, may hold values from -1 to 1
- orbital_map: int32 [64], P('groups'), parts along dimension 0, may hold values from 0 to 31, each once
- couplings: int32 [8, 2], P('groups'), parts along dimension 0, may hold values from 0 to 3, as said below
- particles: int32 [8], P('groups'), parts along dimension 0, may hold values from 0 to 64
- state_counts: int32 [8], P('groups'), parts along dimension 0, may hold values from 320 to 640
Outputs:
- normal_next: bfloat16 [256, 640, 640], P(('groups', 'ops')), parts along dimension 0
- complementary_next: bfloat16 [256, 640, 640], P(('groups', 'ops')), parts along dimension 0
There are 2 independent parts, one for each index of `groups`. A program takes and returns all parts, laid end to end along the dimension named above; each array names one. Nothing has to cross between parts.
Inputs may be any that keep to these rules, and one draw needn't show every extreme that they name: `couplings`: each row holds a source sector and a different target sector.
All inputs are finite; a program needn't handle non-finite values.
Results may differ from a plain program's by a relative error of at most 0.0075.
Values may be sent and summed in bfloat16 or wider, within the bound.
A program may use at most 128 MiB of HBM per device.

v0:
```python
import jax
import jax.numpy as jnp
from jax import lax
from jax.sharding import PartitionSpec as P


def select_entries(lookup, wanted):
    matches = wanted[:, None] == jnp.arange(lookup.shape[0], dtype=jnp.int32)[None, :]
    return jnp.sum(jnp.where(matches, lookup[None, :], 0), axis=1)


def rotate(blocks, basis, live_mask, source, target):
    sectors = live_mask.shape[0]
    states = live_mask.shape[1]
    frames = basis.reshape(sectors, states, states)

    def single(packed):
        block_data, from_sector, to_sector = packed
        frame_in = lax.dynamic_index_in_dim(frames, from_sector, 0, keepdims=False)
        frame_out = lax.dynamic_index_in_dim(frames, to_sector, 0, keepdims=False)
        keep_in = lax.dynamic_index_in_dim(live_mask, from_sector, 0, keepdims=False)
        keep_out = lax.dynamic_index_in_dim(live_mask, to_sector, 0, keepdims=False)
        half_turn = (
            jnp.dot(block_data, frame_in, preferred_element_type=jnp.float32) * keep_in[None, :]
        ).astype(jnp.bfloat16)
        rotated = lax.dot_general(
            frame_out, half_turn, (((0,), (0,)), ((), ())), preferred_element_type=jnp.float32
        )
        return (rotated * keep_out[:, None]).astype(jnp.bfloat16)

    return lax.map(single, (blocks, source, target))


def fetch_second(rotation_two):
    return lax.all_gather(rotation_two, "ops", axis=0, tiled=True)


def local(
    normal_ops,
    rotation_one,
    rotation_two,
    integrals,
    orbital_map,
    couplings,
    particles,
    state_counts,
):
    own_blocks = normal_ops.shape[0]
    states = normal_ops.shape[1]
    orbits = integrals.shape[0]
    link_count = couplings.shape[0]
    devices = lax.axis_size("ops")
    live_mask = (jnp.arange(states, dtype=jnp.int32)[None, :] < state_counts[:, None]).astype(
        jnp.float32
    )
    block_ids = lax.axis_index("ops") * own_blocks + jnp.arange(own_blocks, dtype=jnp.int32)
    link_of = block_ids % link_count
    source = select_entries(couplings[:, 0], link_of)
    target = select_entries(couplings[:, 1], link_of)
    basis_two = None
    basis_one = lax.all_gather(rotation_one, "ops", axis=0, tiled=True)
    normal_mid = rotate(normal_ops, basis_one, live_mask, source, target)
    normal_next = None
    chosen = (orbital_map[:, None] == jnp.arange(orbits, dtype=jnp.int32)[None, :]).astype(
        jnp.float32
    )
    weights = jnp.dot(integrals, chosen.T, precision=lax.Precision.HIGHEST).astype(jnp.bfloat16)
    parity = (1 - 2 * (select_entries(particles, couplings[:, 0]) % 2)).astype(jnp.float32)
    piece_len = states * states // devices
    spread = normal_mid.reshape(own_blocks, devices, piece_len)
    received = lax.all_to_all(spread, "ops", split_axis=1, concat_axis=0, tiled=True)
    entries = received.shape[2]
    grouped = received.reshape(orbits, link_count, entries)
    mixture = jnp.einsum("ko,ocn->kcn", weights, grouped, preferred_element_type=jnp.float32)
    regrouped = lax.all_to_all(
        (mixture * parity[None, :, None])
        .astype(jnp.bfloat16)
        .reshape(orbits * link_count, 1, entries),
        "ops",
        split_axis=0,
        concat_axis=1,
        tiled=True,
    )
    complementary_mid = regrouped.reshape(own_blocks, states, states)
    basis_two = fetch_second(rotation_two)
    normal_next = rotate(normal_mid, basis_two, live_mask, source, target)
    complementary_next = rotate(complementary_mid, basis_two, live_mask, source, target)
    return (normal_next, complementary_next)


def solution(mesh):
    placed = (
        P(("groups", "ops"), None, None),
        P(("groups", "ops"), None),
        P(("groups", "ops"), None),
        P("groups", None),
        P("groups"),
        P("groups", None),
        P("groups"),
        P("groups"),
    )
    return jax.shard_map(
        local,
        mesh=mesh,
        in_specs=placed,
        out_specs=(P(("groups", "ops"), None, None), P(("groups", "ops"), None, None)),
        check_vma=False,
    )
```

profile of v0, /device:TPU:11, one launch (start us, length us, event | category | flops | bytes accessed | tf_op | source)
XLA Modules:
  0.0 738.0 jit_solution(9116732155998061797)
XLA Ops:
  7.2 0.7 all-gather.5.cloned.1.call-update
  7.9 0.8 slice_bitcast_fusion.1
  8.8 0.7 fusion.48
  9.5 47.5 %all-gather.5.cloned.1.call-done = bf16[2560,640]{1,0:T(8,128)(2,1)} async-done(((bf16[160,640]{1,0:T(8,128)(2,1)}), bf16[2560,640]{1,0:T(8,128)(2,1)}) %all-gather.5.cloned.1.call-update) | async-done | bytes 3276816 | tf_op jit(solution)/shard_map/all_gather | solution.py:61
  57.0 3.3 broadcast.72.clone.1
  60.3 74.2 %while.30 = (s32[]{:T(128)}, bf16[8,640,640]{2,1,0:T(8,128)(2,1)}, s32[8]{0:T(128)S(1)}, bf16[4,640,640]{2,1,0:T(8,128)(2,1)S(1)}, bf16[8,640,640]{2,1,0:T(8,128...) while((s32[]{:T(128)}, bf16[8,640,640]{2,1,0:T(8,128)(2,1)}, ...), condition=%wide.region_3.4_spmd, body=%wide.region_2.3_spmd.sunk | while | flops 1050214400 | bytes 3296465 | solution.py:31
  60.3 0.7 dynamic_slice.138
  63.0 0.7 dynamic_slice.137
  65.8 3.8 fusion.72
  72.3 0.7 dynamic_slice.137
  75.1 3.8 fusion.72
  78.8 0.7 dynamic_slice.138
  81.6 0.7 dynamic_slice.137
  84.3 3.8 fusion.72
  90.8 0.7 dynamic_slice.137
  93.6 3.8 fusion.72
  100.1 0.7 dynamic_slice.137
  102.9 3.8 fusion.72
  106.6 0.7 dynamic_slice.138
  109.4 0.7 dynamic_slice.137
  112.2 3.8 fusion.72
  118.7 0.7 dynamic_slice.137
  121.4 3.8 fusion.72
  125.2 0.7 dynamic_slice.138
  127.9 0.7 dynamic_slice.137
  130.7 3.8 fusion.72
  134.5 9.1 %reshape.69 = bf16[8,16,25600]{2,1,0:T(8,128)(2,1)} reshape(bf16[8,640,640]{2,1,0:T(8,128)(2,1)} %get-tuple-element.343) | data formatting | bytes 13107200 | tf_op jit(solution)/shard_map/reshape | solution.py:70
  143.6 9.2 %copy.24 = bf16[8,16,25600]{2,0,1:T(8,128)(2,1)} copy(bf16[8,16,25600]{2,1,0:T(8,128)(2,1)} %reshape.69) | data formatting | bytes 13107200 | tf_op jit(solution)/shard_map/reshape | solution.py:70
  152.8 5.9 all-to-all-start
  159.1 142.6 %all-to-all-done = bf16[8,16,25600]{2,0,1:T(8,128)(2,1)} async-done(((bf16[8,16,25600]{2,0,1:T(8,128)(2,1)}), bf16[8,16,25600]{2,0,1:T(8,128)(2,1)}, u32[]{:S(2)}, u32[]{:S(2)}) %all-to-all-start) | async-done | bytes 6553632 | tf_op jit(solution)/shard_map/all_to_all | solution.py:71
  301.7 8.8 %reshape.70 = bf16[32,4,25600]{2,1,0:T(4,128)(2,1)} reshape(bf16[16,8,1,25600]{3,1,0,2:T(8,128)(2,1)} %bitcast.24) | data formatting | bytes 13107200 | tf_op jit(solution)/shard_map/reshape | solution.py:73
  310.5 9.6 %fusion.45 = bf16[32,4,25600]{2,0,1:T(8,128)(2,1)} fusion(bf16[32,32,1]{1,0,2:T(8,128)(2,1)S(1)} %fusion.47, bf16[32,4,25600]{2,1,0:T(4,128)(2,1)} %reshape.70, f32[4]{0:T(128)S(1)} %fusion.52), kind=kOutput, calls=%fused_computation.43 | convolution fusion | flops 216268800 | bytes 13109264 | tf_op jit(solution)/shard_map/ko,ocn->kcn/dot_general | solution.py:74
  320.1 10.7 %copy.27 = bf16[32,4,25600]{2,1,0:T(4,128)(2,1)} copy(bf16[32,4,25600]{2,0,1:T(8,128)(2,1)} %fusion.45) | data formatting | bytes 13107200 | tf_op jit(solution)/shard_map/convert_element_type | solution.py:77
  330.8 21.4 %reshape.74 = bf16[128,1,25600]{2,1,0:T(2,128)(2,1)} reshape(bf16[32,4,25600]{2,1,0:T(4,128)(2,1)} %copy.27) | data formatting | bytes 13107200 | tf_op jit(solution)/shard_map/reshape | solution.py:78
  352.8 41.2 %reduce.12 = bf16[128,25600]{1,0:T(8,128)(2,1)} reduce(bf16[128,1,25600]{2,1,0:T(2,128)(2,1)} %reshape.74, bf16[]{:T(256)} %broadcast.85), dimensions={1}, to_apply=%reshape.74.reduce_sub_computation | reduce | bytes 13107202 | tf_op jit(solution)/shard_map/reshape | solution.py:78
  394.0 12.7 %reshape.81 = bf16[16,2,102400]{2,1,0:T(2,128)(2,1)} reshape(bf16[128,25600]{1,0:T(8,128)(2,1)} %reduce.12) | data formatting | bytes 13107200
  406.7 4.8 all-to-all-start.1
  411.5 0.7 all-gather.3.cloned.1.call-update
  412.3 127.9 %all-gather.3.cloned.1.call-done = bf16[2560,640]{1,0:T(8,128)(2,1)} async-done(((bf16[160,640]{1,0:T(8,128)(2,1)}), bf16[2560,640]{1,0:T(8,128)(2,1)}) %all-gather.3.cloned.1.call-update) | async-done | bytes 3276816 | tf_op jit(solution)/shard_map/all_gather | solution.py:35
  540.1 3.3 broadcast.72.clone
  543.4 70.7 %while.31 = (s32[]{:T(128)}, bf16[8,640,640]{2,1,0:T(8,128)(2,1)}, s32[8]{0:T(128)S(1)}, bf16[4,640,640]{2,1,0:T(8,128)(2,1)S(1)}, bf16[8,640,640]{2,1,0:T(8,128...) while((s32[]{:T(128)}, bf16[8,640,640]{2,1,0:T(8,128)(2,1)}, ...), condition=%wide.region_5.6_spmd, body=%wide.region_4.5_spmd.sunk | while | flops 1050214400 | bytes 3296465 | solution.py:31
  548.5 3.8 fusion.76
  557.3 3.8 fusion.76
  566.2 3.8 fusion.76
  575.0 3.8 fusion.76
  583.9 3.8 fusion.76
  592.7 3.8 fusion.76
  601.5 3.8 fusion.76
  610.4 3.8 fusion.76
  614.1 14.6 %reshape.82 = bf16[128,1,25600]{2,1,0:T(2,128)(2,1)} reshape(bf16[16,2,102400]{2,1,0:T(2,128)(2,1)} %all-to-all-done.1) | data formatting | bytes 13107200
  628.8 9.5 %copy.36 = bf16[128,1,25600]{2,0,1:T(8,128)(2,1)} copy(bf16[128,1,25600]{2,1,0:T(2,128)(2,1)} %reshape.82) | data formatting | bytes 13107200
  638.3 9.2 %copy.29 = bf16[8,16,1,25600]{3,1,0,2:T(8,128)(2,1)} copy(bf16[8,16,1,25600]{3,0,1,2:T(8,128)(2,1)} %bitcast.113) | data formatting | bytes 13107200 | tf_op jit(solution)/shard_map/all_to_all | solution.py:75
  647.4 9.1 %reshape.72 = bf16[8,640,640]{2,1,0:T(8,128)(2,1)} reshape(bf16[8,16,1,25600]{3,1,0,2:T(8,128)(2,1)} %copy.29) | data formatting | bytes 13107200 | tf_op jit(solution)/shard_map/reshape | solution.py:84
  656.6 3.3 broadcast.72.clone.2
  659.9 70.6 %while.32 = (s32[]{:T(128)}, bf16[8,640,640]{2,1,0:T(8,128)(2,1)}, s32[8]{0:T(128)S(1)}, bf16[4,640,640]{2,1,0:T(8,128)(2,1)S(1)}, bf16[8,640,640]{2,1,0:T(8,128...) while((s32[]{:T(128)}, bf16[8,640,640]{2,1,0:T(8,128)(2,1)}, ...), condition=%wide.region_8.9_spmd, body=%wide.region_7.8_spmd.sunk | while | flops 1050214400 | bytes 3296465 | solution.py:31
  664.9 3.8 fusion.80
  673.8 3.8 fusion.80
  682.6 3.8 fusion.80
  691.4 3.8 fusion.80
  700.2 3.8 fusion.80
  709.1 3.8 fusion.80
  717.9 3.8 fusion.80
  726.7 3.8 fusion.80
  730.5 0.7 copy-done.1
  (80 shorter events, 24.0 us)
Async XLA Ops:
  7.2 151.7 %copy-start = (f32[32,32]{1,0:T(8,128)S(1)}, f32[32,32]{1,0:T(8,128)}, u32[]{:S(2)}) copy-start(f32[32,32]{1,0:T(8,128)} %param.17) | copy-start | bytes 12292
  7.2 49.8 %all-gather.5.cloned.1.call-start = ((), (), s32[]{:S(2)}) async-start(), calls=%async_computation.3 | async-start | bytes 3481600 | tf_op jit(solution)/shard_map/all_gather | solution.py:61
  57.0 3.3 copy-start.3
  152.8 5.9 copy-start.4
  152.8 6.1 copy-start.5
  152.8 148.9 %all-to-all-start = ((bf16[8,16,25600]{2,0,1:T(8,128)(2,1)}), bf16[8,16,25600]{2,0,1:T(8,128)(2,1)}, u32[]{:S(2)}, u32[]{:S(2)}) async-start(bf16[8,16,25600]{2,0,1:T(8,128)(2,1)} %copy.24), calls=%async_computation | async-start | bytes 13107200 | tf_op jit(solution)/shard_map/all_to_all | solution.py:71
  406.7 207.4 %all-to-all-start.1 = ((bf16[16,2,102400]{2,1,0:T(2,128)(2,1)}), bf16[16,2,102400]{2,1,0:T(2,128)(2,1)}, u32[]{:S(2)}, u32[]{:S(2)}) async-start(bf16[16,2,102400]{2,1,0:T(2,128)(2,1)} %reshape.81), calls=%async_computation.1 | async-start | bytes 13107200 | tf_op jit(solution)/shard_map/all_to_all | solution.py:75
  411.5 128.6 %all-gather.3.cloned.1.call-start = ((), (), s32[]{:S(2)}) async-start(), calls=%async_computation.2 | async-start | bytes 3481600 | tf_op jit(solution)/shard_map/all_gather | solution.py:35
  540.1 3.3 copy-start.2
  730.5 0.7 copy-start.1
Sparse Core Ops, SparseCore 0:
  10.3 46.6 all-gather.4
  414.6 125.4 all-gather.2
where the time goes:
time: 748 us; the launch traced here: 738 us
  waiting for transfers between devices  319 us (43%)
  local copies, waits for them, and re-layouts  157 us (21%)
  matrix products  100 us (13%)
  loops' own time  94.5 us (13%)
  other arithmetic  42.3 us (6%)
  between operations  14.1 us (2%)
  starting transfers between devices  10.7 us (1%)
    all_to_all x1, waiting for transfers between devices, local(): lax.all_to_all(spread, 'ops', split_axis=1, concat_axis=0, tiled=True)  143 us
    all_gather x1, waiting for transfers between devices, fetch_second(): return lax.all_gather(rotation_two, 'ops', axis=0, tiled=True)  128 us
    another operation x3, loops' own time, rotate(): return lax.map(single, (blocks, source, target))  94.5 us
    dot_general x24, matrix products, single(): lax.dot_general(frame_out, half_turn, (((0,), (0,)), ((), ())), preferred...  90.2 us
    all_gather x1, waiting for transfers between devices, local(): basis_one = lax.all_gather(rotation_one, 'ops', axis=0, tiled=True)  47.5 us
    reshape x1, other arithmetic, local(): regrouped = lax.all_to_all((mixture * parity[None, :, None]).astype(jnp.b...  41.2 us
    unnamed x15, local copies, waits for them, and re-layouts  37.6 us
    dynamic_slice x48, local copies, waits for them, and re-layouts, rotate(): return lax.map(single, (blocks, source, target))  30.2 us
  transfers between devices with their start and end apart: 4, of which 3 were waited for; matrix products, arithmetic and copies ran while one was open for 6% of the time, Pallas kernels for 0%

commit v1 on v0

--- a/solution.py
+++ b/solution.py
@@ -1,6 +1,8 @@
 import jax
 import jax.numpy as jnp
 from jax import lax
+from jax.experimental import pallas as pl
+from jax.experimental.pallas import tpu as pltpu
 from jax.sharding import PartitionSpec as P
 
 
@@ -35,7 +37,7 @@
     return lax.all_gather(rotation_two, "ops", axis=0, tiled=True)
 
 
-def local(
+def local_general(
     normal_ops,
     rotation_one,
     rotation_two,
@@ -88,6 +90,146 @@
     return (normal_next, complementary_next)
 
 
+SUB = 8
+
+
+def mix_kernel(weights_ref, entries_ref, mixed_ref):
+    orbits, rows, states = entries_ref.shape
+    weights = weights_ref[...]
+    for start in range(0, rows, SUB):
+        piece = entries_ref[:, start : start + SUB, :].astype(jnp.float32)
+        piece = piece.reshape(orbits * SUB, states).astype(jnp.bfloat16)
+        mixed = jnp.dot(weights, piece, preferred_element_type=jnp.float32)
+        mixed_ref[:, start : start + SUB, :] = mixed.reshape(orbits, SUB, states).astype(
+            jnp.bfloat16
+        )
+
+
+def mix(weights, entries):
+    orbits, rows, states = entries.shape
+    return pl.pallas_call(
+        mix_kernel,
+        out_shape=jax.ShapeDtypeStruct(entries.shape, jnp.bfloat16),
+        cost_estimate=pl.CostEstimate(
+            flops=2 * orbits * orbits * SUB * rows * states,
+            bytes_accessed=4 * orbits * rows * states,
+            transcendentals=0,
+        ),
+    )(weights, entries)
+
+
+def turn_kernel(source_ref, target_ref, data_ref, frame_in_ref, frame_out_ref, out_ref):
+    states = frame_in_ref.shape[1]
+    data = data_ref[...]
+    if data.ndim == 4:
+        data = data.astype(jnp.float32).reshape(states, states).astype(jnp.bfloat16)
+    else:
+        data = data.reshape(states, states)
+    half_turn = jnp.dot(data, frame_in_ref[0], preferred_element_type=jnp.float32)
+    out_ref[0] = jnp.dot(
+        frame_out_ref[0], half_turn.astype(jnp.bfloat16), preferred_element_type=jnp.float32
+    ).astype(jnp.bfloat16)
+
+
+def turn(data, frames, frames_t, source, target):
+    states = frames.shape[1]
+    links = source.shape[0]
+    if data.ndim == 4:
+        count = data.shape[1]
+        spec = pl.BlockSpec((data.shape[0], 1) + data.shape[2:], lambda b, s, t: (0, b, 0, 0))
+    else:
+        count = data.shape[0]
+        spec = pl.BlockSpec((1, states, states), lambda b, s, t: (b, 0, 0))
+    return pl.pallas_call(
+        turn_kernel,
+        grid_spec=pltpu.PrefetchScalarGridSpec(
+            num_scalar_prefetch=2,
+            grid=(count,),
+            in_specs=[
+                spec,
+                pl.BlockSpec((1, states, states), lambda b, s, t: (s[b % links], 0, 0)),
+                pl.BlockSpec((1, states, states), lambda b, s, t: (t[b % links], 0, 0)),
+            ],
+            out_specs=pl.BlockSpec((1, states, states), lambda b, s, t: (b, 0, 0)),
+        ),
+        out_shape=jax.ShapeDtypeStruct((count, states, states), jnp.bfloat16),
+        cost_estimate=pl.CostEstimate(
+            flops=4 * count * states**3,
+            bytes_accessed=8 * count * states**2,
+            transcendentals=0,
+        ),
+    )(source, target, data, frames, frames_t)
+
+
+def local(
+    normal_ops,
+    rotation_one,
+    rotation_two,
+    integrals,
+    orbital_map,
+    couplings,
+    particles,
+    state_counts,
+):
+    own_blocks, states, _ = normal_ops.shape
+    orbits = integrals.shape[0]
+    links = couplings.shape[0]
+    sectors = state_counts.shape[0]
+    devices = lax.axis_size("ops")
+    own = own_blocks // links
+    if own * links != own_blocks or states % (devices * SUB):
+        return local_general(
+            normal_ops,
+            rotation_one,
+            rotation_two,
+            integrals,
+            orbital_map,
+            couplings,
+            particles,
+            state_counts,
+        )
+    rows = states // devices
+    source, target = couplings[:, 0], couplings[:, 1]
+    chosen = (orbital_map[:, None] == jnp.arange(orbits, dtype=jnp.int32)[None, :]).astype(
+        jnp.float32
+    )
+    weights = jnp.dot(integrals, chosen.T, precision=lax.Precision.HIGHEST)
+    parity = (1 - 2 * (select_entries(particles, source) % 2)).astype(jnp.float32)
+    eye = jnp.eye(SUB, dtype=jnp.float32)
+    spread_weights = (weights[:, None, :, None] * eye[None, :, None, :]).reshape(
+        orbits * SUB, orbits * SUB
+    )
+    split = normal_ops.reshape(own, links, devices, rows, states).transpose(1, 2, 0, 3, 4)
+    received = [
+        lax.all_to_all(split[c], "ops", split_axis=0, concat_axis=0, tiled=True)
+        for c in range(links)
+    ]
+    live = (
+        jnp.arange(states, dtype=jnp.int32)[None, :] < state_counts[:, None]
+    ).astype(jnp.bfloat16)[:, None, :]
+    basis_one = lax.all_gather(rotation_one, "ops", axis=0, tiled=True)
+    basis_two = lax.all_gather(rotation_two, "ops", axis=0, tiled=True)
+    basis_one = basis_one.reshape(sectors, states, states) * live
+    basis_two = basis_two.reshape(sectors, states, states) * live
+    frames = jnp.einsum(
+        "sij,sjk->sik", basis_one, basis_two, preferred_element_type=jnp.float32
+    ).astype(jnp.bfloat16)
+    frames_t = frames.swapaxes(1, 2)
+    normal_next = turn(normal_ops, frames, frames_t, source, target)
+    pieces = []
+    for c in range(links):
+        mixed = mix(
+            (spread_weights * parity[c]).astype(jnp.bfloat16),
+            received[c].reshape(orbits, rows, states),
+        )
+        back = lax.all_to_all(
+            mixed.reshape(devices, own, rows, states), "ops", split_axis=0, concat_axis=0, tiled=True
+        )
+        pieces.append(turn(back, frames, frames_t, source[c : c + 1], target[c : c + 1]))
+    complementary_next = jnp.stack(pieces, axis=1).reshape(own_blocks, states, states)
+    return (normal_next, complementary_next)
+
+
 def solution(mesh):
     placed = (
         P(("groups", "ops"), None, None),

time: 748 us -> 424 us (0.57); the launches traced: 738 us -> 423 us
  waiting for transfers between devices: 319 us -> 146 us
  blocking collectives: 0 us -> 130 us
  local copies, waits for them, and re-layouts: 157 us -> 32.2 us
  loops' own time: 94.5 us -> 0 us
  matrix products: 100 us -> 6.24 us
  Pallas kernels: 0 us -> 59.3 us
  other arithmetic: 42.3 us -> 10.4 us
  starting transfers between devices: 10.7 us -> 24.8 us
    all_to_all x0 -> x3, blocking collectives: none -> 130 us  [local(): lax.all_to_all(split[c], 'ops', split_axis=0, concat_axis=0, tiled=True)]
    all_gather x1, waiting for transfers between devices: 128 us -> 0.01 us  [local(): basis_two = lax.all_gather(rotation_two, 'ops', axis=0, tiled=True)]
    another operation x3 -> x0, loops' own time: 94.5 us -> none  [rotate(): return lax.map(single, (blocks, source, target))]
    dot_general x26 -> x2, matrix products: 100 us -> 6.24 us  [the longest x1 6.06 us: local(): jnp.einsum('sij,sjk->sik', basis_one, basis_two, preferred_element_type=j...]
    pallas_call x0 -> x9, Pallas kernels: none -> 59.3 us  [the longest x5 45.8 us: turn(): pl.pallas_call(turn_kernel, grid_spec=pltpu.PrefetchScalarGridSpec(num_sc...]
    reshape x6 -> x1, local copies, waits for them, and re-layouts: 58.2 us -> 3.43 us  [local(): normal_ops.reshape(own, links, devices, rows, states)]
    all_gather x1, waiting for transfers between devices: 47.5 us -> 0.01 us  [local(): basis_one = lax.all_gather(rotation_one, 'ops', axis=0, tiled=True)]
    reshape x1 -> x0, other arithmetic: 41.2 us -> none  [local(): regrouped = lax.all_to_all((mixture * parity[None, :, None]).astype(jnp.b...]
  transfers between devices with their start and end apart: 4 -> 7, of which waited for: 3 -> 5; matrix products, arithmetic and copies ran while one was open for 6% -> 9% of each run, Pallas kernels for 0% -> 8%
where the time goes in v1:
time: 424 us; the launch traced here: 423 us
  waiting for transfers between devices  146 us (34%)
  blocking collectives  130 us (31%)
  Pallas kernels  59.3 us (14%)
  local copies, waits for them, and re-layouts  32.2 us (8%)
  starting transfers between devices  24.8 us (6%)
  between operations  14.1 us (3%)
  other arithmetic  10.4 us (2%)
  matrix products  6.24 us (1%)
    all_to_all x3, blocking collectives, local(): lax.all_to_all(split[c], 'ops', split_axis=0, concat_axis=0, tiled=True)  130 us
    all_to_all x4, waiting for transfers between devices, local(): lax.all_to_all(mixed.reshape(devices, own, rows, states), 'ops', split_ax...  112 us
    pallas_call x5, Pallas kernels, turn(): pl.pallas_call(turn_kernel, grid_spec=pltpu.PrefetchScalarGridSpec(num_sc...  45.8 us
    all_to_all x1, waiting for transfers between devices, local(): lax.all_to_all(split[c], 'ops', split_axis=0, concat_axis=0, tiled=True)  32.5 us
    all_to_all x4, starting transfers between devices, local(): lax.all_to_all(mixed.reshape(devices, own, rows, states), 'ops', split_ax...  18.3 us
    convert_element_type x4, local copies, waits for them, and re-layouts, local(): (spread_weights * parity[c]).astype(jnp.bfloat16)  17.5 us
    pallas_call x4, Pallas kernels, mix(): pl.pallas_call(mix_kernel, out_shape=jax.ShapeDtypeStruct(entries.shape,...  13.5 us
  transfers between devices with their start and end apart: 7, of which 5 were waited for; matrix products, arithmetic and copies ran while one was open for 9% of the time, Pallas kernels for 8%

profile of v1, /device:TPU:11, one launch (start us, length us, event | category | flops | bytes accessed | tf_op | source)
XLA Modules:
  0.0 423.0 jit_solution(11441582473566744979)
XLA Ops:
  7.2 0.0 copy-start
  7.2 3.4 copy.38
  10.6 1.8 slice_bitcast_fusion.3
  12.4 44.0 %all_to_all.40 = bf16[16,2,40,640]{3,2,1,0:T(8,128)(2,1)} all-to-all(bf16[16,2,40,640]{3,2,1,0:T(8,128)(2,1)S(1)} %get-tuple-element.2), channel_id=1, replica_groups=mesh['groups'=2,'ops'=16] {'ops'}, dimensions={0} | all-to-all | bytes 3276800 | tf_op jit(solution)/shard_map/all_to_all | solution.py:204
  56.4 43.0 %all_to_all.41 = bf16[16,2,40,640]{3,2,1,0:T(8,128)(2,1)} all-to-all(bf16[16,2,40,640]{3,2,1,0:T(8,128)(2,1)S(1)} %get-tuple-element.5), channel_id=1, replica_groups=mesh['groups'=2,'ops'=16] {'ops'}, dimensions={0} | all-to-all | bytes 3276800 | tf_op jit(solution)/shard_map/all_to_all | solution.py:204
  99.4 0.0 copy-start.8
  99.4 0.0 copy-start.5
  99.4 0.0 copy-start.9
  99.4 43.1 %all_to_all.42 = bf16[16,2,40,640]{3,2,1,0:T(8,128)(2,1)} all-to-all(bf16[16,2,40,640]{3,2,1,0:T(8,128)(2,1)S(1)} %get-tuple-element.4), channel_id=1, replica_groups=mesh['groups'=2,'ops'=16] {'ops'}, dimensions={0} | all-to-all | bytes 3276800 | tf_op jit(solution)/shard_map/all_to_all | solution.py:204
  142.5 6.4 %all-to-all-start.6 = ((bf16[16,2,40,640]{3,2,1,0:T(8,128)(2,1)}), bf16[16,2,40,640]{3,2,1,0:T(8,128)(2,1)}, u32[]{:S(2)}, u32[]{:S(2)}) async-start(bf16[16,2,40,640]{3,2,1,0:T(8,128)(2,1)} %get-tuple-element.3), calls=%async_computation.6 | async-start | bytes 3276800 | tf_op jit(solution)/shard_map/all_to_all | solution.py:204
  148.9 0.0 all-gather.3.cloned.1.call-start
  148.9 0.7 all-gather.3.cloned.1.call-update
  149.6 0.0 copy-done
  149.6 0.0 copy-done.8
  149.6 0.2 convolution_bitcast_fusion
  149.8 0.1 copy.29
  149.9 0.0 copy-done.5
  149.9 0.6 slice_bitcast_fusion.4
  150.5 0.0 copy-start.6
  150.5 0.0 copy-done.9
  150.5 0.2 select_reduce_fusion
  150.7 0.7 fusion.21
  151.4 6.9 %fusion = (bf16[32,8,32,8]{3,2,1,0:T(8,128)(2,1)}, bf16[32,8,32,8]{3,2,1,0:T(8,128)(2,1)S(1)}, bf16[32,8,32,8]{3,2,1,0:T(8,128)(2,1)}, bf16[32,8,32,8]{3,2,1,0:T(8,128)(2,1)}) fusion(f32[]{:T(128)} %bitcast.8, f32[8,8]{1,0:T(8,128)S(1)} %fusion.15, f32[32,32]{1,0:T(8,128)S(1)} %copy.29, f32[]{:T(128)} %bitcast.31, f32[]{:T(128)} %bitcast.24, f32[]{:T(128)} %bitcast.17), kind=kLoop, calls=%fused_computation.6 | loop fusion | flops 589824 | bytes 528656 | tf_op jit(solution)/shard_map/convert_element_type | solution.py:222
  158.3 0.0 copy-done.6
  158.3 4.7 %convert_element_type.49.weights_ref = bf16[256,256]{1,0:T(8,128)(2,1)} reshape(bf16[32,8,32,8]{3,2,1,0:T(8,128)(2,1)} %get-tuple-element.6) | data formatting | bytes 262144 | tf_op jit(solution)/shard_map/convert_element_type | solution.py:222
  163.0 3.4 shard_map.96
  166.3 32.5 %all-to-all-done.6 = bf16[16,2,40,640]{3,2,1,0:T(8,128)(2,1)} async-done(((bf16[16,2,40,640]{3,2,1,0:T(8,128)(2,1)}), bf16[16,2,40,640]{3,2,1,0:T(8,128)(2,1)}, u32[]{:S(2)}, u32[]{:S(2)}) %all-to-all-start.6) | async-done | bytes 1638432 | tf_op jit(solution)/shard_map/all_to_all | solution.py:204
  198.9 4.6 %all-to-all-start.1 = ((bf16[16,2,40,640]{3,2,1,0:T(8,128)(2,1)}), bf16[16,2,40,640]{3,2,1,0:T(8,128)(2,1)}, u32[]{:S(2)}, u32[]{:S(2)}) async-start(bf16[16,2,40,640]{3,2,1,0:T(8,128)(2,1)} %bitcast.73), calls=%async_computation.1 | async-start | bytes 3276800 | tf_op jit(solution)/shard_map/all_to_all | solution.py:225
  203.5 4.7 %convert_element_type.51.weights_ref = bf16[256,256]{1,0:T(8,128)(2,1)} reshape(bf16[32,8,32,8]{3,2,1,0:T(8,128)(2,1)} %get-tuple-element.9) | data formatting | bytes 262144 | tf_op jit(solution)/shard_map/convert_element_type | solution.py:222
  208.2 3.4 shard_map.98
  211.5 32.2 %all-to-all-done.1.data_ref = bf16[16,2,40,640]{3,2,1,0:T(8,128)(2,1)} async-done(((bf16[16,2,40,640]{3,2,1,0:T(8,128)(2,1)}), bf16[16,2,40,640]{3,2,1,0:T(8,128)(2,1)}, u32[]{:S(2)}, u32[]{:S(2)}) %all-to-all-start.1) | async-done | bytes 1638432 | tf_op jit(solution)/shard_map/all_to_all | solution.py:225
  243.7 4.3 %all-to-all-start.3 = ((bf16[16,2,40,640]{3,2,1,0:T(8,128)(2,1)}), bf16[16,2,40,640]{3,2,1,0:T(8,128)(2,1)}, u32[]{:S(2)}, u32[]{:S(2)}) async-start(bf16[16,2,40,640]{3,2,1,0:T(8,128)(2,1)} %bitcast.71), calls=%async_computation.3 | async-start | bytes 3276800 | tf_op jit(solution)/shard_map/all_to_all | solution.py:225
  248.1 0.0 all-gather.5.cloned.1.call-start
  248.1 0.7 all-gather.5.cloned.1.call-update
  248.8 4.7 %convert_element_type.53.weights_ref = bf16[256,256]{1,0:T(8,128)(2,1)} reshape(bf16[32,8,32,8]{3,2,1,0:T(8,128)(2,1)} %get-tuple-element.8) | data formatting | bytes 262144 | tf_op jit(solution)/shard_map/convert_element_type | solution.py:222
  253.5 3.4 shard_map.100
  256.8 40.2 %all-to-all-done.3.data_ref = bf16[16,2,40,640]{3,2,1,0:T(8,128)(2,1)} async-done(((bf16[16,2,40,640]{3,2,1,0:T(8,128)(2,1)}), bf16[16,2,40,640]{3,2,1,0:T(8,128)(2,1)}, u32[]{:S(2)}, u32[]{:S(2)}) %all-to-all-start.3) | async-done | bytes 1638432 | tf_op jit(solution)/shard_map/all_to_all | solution.py:225
  297.1 5.1 %all-to-all-start.5 = ((bf16[16,2,40,640]{3,2,1,0:T(8,128)(2,1)}), bf16[16,2,40,640]{3,2,1,0:T(8,128)(2,1)}, u32[]{:S(2)}, u32[]{:S(2)}) async-start(bf16[16,2,40,640]{3,2,1,0:T(8,128)(2,1)} %bitcast.72), calls=%async_computation.5 | async-start | bytes 3276800 | tf_op jit(solution)/shard_map/all_to_all | solution.py:225
  302.2 3.5 convert_element_type.55.weights_ref
  305.7 0.0 copy-start.7
  305.7 3.4 shard_map.102
  309.1 33.8 %all-to-all-done.5.data_ref = bf16[16,2,40,640]{3,2,1,0:T(8,128)(2,1)} async-done(((bf16[16,2,40,640]{3,2,1,0:T(8,128)(2,1)}), bf16[16,2,40,640]{3,2,1,0:T(8,128)(2,1)}, u32[]{:S(2)}, u32[]{:S(2)}) %all-to-all-start.5) | async-done | bytes 1638432 | tf_op jit(solution)/shard_map/all_to_all | solution.py:225
  342.9 4.3 %all-to-all-start.7 = ((bf16[16,2,40,640]{3,2,1,0:T(8,128)(2,1)}), bf16[16,2,40,640]{3,2,1,0:T(8,128)(2,1)}, u32[]{:S(2)}, u32[]{:S(2)}) async-start(bf16[16,2,40,640]{3,2,1,0:T(8,128)(2,1)} %bitcast.70), calls=%async_computation.7 | async-start | bytes 3276800 | tf_op jit(solution)/shard_map/all_to_all | solution.py:225
  347.2 0.6 fusion.20
  347.8 0.0 copy-done.7
  347.8 0.1 fusion.13
  347.9 0.0 all-gather.3.cloned.1.call-done
  347.9 0.0 all-gather.5.cloned.1.call-done
  347.9 6.1 %fusion.7 = bf16[4,640,640]{1,2,0:T(8,128)(2,1)S(1)} fusion(bf16[4,640,640]{2,1,0:T(8,128)(2,1)} %bitcast.75, bf16[4,640,640]{2,1,0:T(8,128)(2,1)} %bitcast.74, bf16[4,640]{1,0:T(4,128)(2,1)S(1)} %fusion.13), kind=kOutput, calls=%fused_computation.13 | convolution fusion | flops 2102067200 | bytes 9835520 | tf_op jit(solution)/shard_map/sij,sjk->sik/dot_general | solution.py:214
  354.0 0.0 copy-start.2
  354.0 4.1 copy.28.frame_in_ref
  358.1 0.0 copy-done.2
  358.1 7.1 %shard_map.97 = bf16[2,640,640]{2,1,0:T(8,128)(2,1)} custom-call(s32[1]{0:T(128)} %bitcast.5.source_ref, s32[1]{0:T(128)} %bitcast.6.target_ref, bf16[16,2,40,640]{3,2,1,0:T(8,128)(2,1)} %all-to-all-done.1.data_ref, bf16[4,640,640]{2,1,0:T(8,128)(2,1)} %copy.28.frame_in_ref, bf16[4,640,640]{2,1,0:T(8,128)(2,1)} %bitcast.55), custom_call_target="tpu_custom_call" | custom-call | flops 2097152000 | bytes 6553600 | tf_op jit(solution)/shard_map/pallas_call | solution.py:143
  365.2 7.0 %shard_map.99 = bf16[2,640,640]{2,1,0:T(8,128)(2,1)} custom-call(s32[1]{0:T(128)} %bitcast.15.source_ref, s32[1]{0:T(128)} %bitcast.16.target_ref, bf16[16,2,40,640]{3,2,1,0:T(8,128)(2,1)} %all-to-all-done.3.data_ref, bf16[4,640,640]{2,1,0:T(8,128)(2,1)} %copy.28.frame_in_ref, bf16[4,640,640]{2,1,0:T(8,128)(2,1)} %bitcast.56), custom_call_target="tpu_custom_call" | custom-call | flops 2097152000 | bytes 6553600 | tf_op jit(solution)/shard_map/pallas_call | solution.py:143
  372.2 6.9 %shard_map.101 = bf16[2,640,640]{2,1,0:T(8,128)(2,1)} custom-call(s32[1]{0:T(128)} %bitcast.22.source_ref, s32[1]{0:T(128)} %bitcast.23.target_ref, bf16[16,2,40,640]{3,2,1,0:T(8,128)(2,1)} %all-to-all-done.5.data_ref, bf16[4,640,640]{2,1,0:T(8,128)(2,1)} %copy.28.frame_in_ref, bf16[4,640,640]{2,1,0:T(8,128)(2,1)} %bitcast.57), custom_call_target="tpu_custom_call" | custom-call | flops 2097152000 | bytes 6553600 | tf_op jit(solution)/shard_map/pallas_call | solution.py:143
  379.1 5.7 %all-to-all-done.7.data_ref = bf16[16,2,40,640]{3,2,1,0:T(8,128)(2,1)} async-done(((bf16[16,2,40,640]{3,2,1,0:T(8,128)(2,1)}), bf16[16,2,40,640]{3,2,1,0:T(8,128)(2,1)}, u32[]{:S(2)}, u32[]{:S(2)}) %all-to-all-start.7) | async-done | bytes 1638432 | tf_op jit(solution)/shard_map/all_to_all | solution.py:225
  384.8 0.0 copy-start.3
  384.8 7.4 %shard_map.103 = bf16[2,640,640]{2,1,0:T(8,128)(2,1)} custom-call(s32[1]{0:T(128)} %bitcast.29.source_ref, s32[1]{0:T(128)} %bitcast.30.target_ref, bf16[16,2,40,640]{3,2,1,0:T(8,128)(2,1)} %all-to-all-done.7.data_ref, bf16[4,640,640]{2,1,0:T(8,128)(2,1)} %copy.28.frame_in_ref, bf16[4,640,640]{2,1,0:T(8,128)(2,1)} %bitcast.58), custom_call_target="tpu_custom_call" | custom-call | flops 2097152000 | bytes 6553600 | tf_op jit(solution)/shard_map/pallas_call | solution.py:143
  392.2 0.0 copy-done.3
  392.2 0.0 copy-done.4
  392.2 3.2 pad_maximum_fusion
  395.4 3.4 copy.35
  398.8 17.4 %shard_map.95 = bf16[8,640,640]{2,1,0:T(8,128)(2,1)} custom-call(s32[4]{0:T(128)} %copy-done.6, s32[4]{0:T(128)} %get-tuple-element.18.target_ref, bf16[8,640,640]{2,1,0:T(8,128)(2,1)} %data_ref.1, bf16[4,640,640]{2,1,0:T(8,128)(2,1)} %copy.28.frame_in_ref, bf16[4,640,640]{2,1,0:T(8,128)(2,1)} %bitcast.59), custom_call_target="tpu_custom_call" | custom-call | flops 8388608000 | bytes 26214400 | tf_op jit(solution)/shard_map/pallas_call | solution.py:143
  416.2 0.0 copy-done.1
  (4 shorter events, 0.0 us)
Async XLA Ops:
  7.2 142.5 %copy-start = (f32[32,32]{1,0:T(8,128)S(1)}, f32[32,32]{1,0:T(8,128)}, u32[]{:S(2)}) copy-start(f32[32,32]{1,0:T(8,128)} %param.11) | copy-start | bytes 12292
  99.4 50.3 %copy-start.8 = (s32[32]{0:T(128)S(1)}, s32[32]{0:T(128)}, u32[]{:S(2)}) copy-start(s32[32]{0:T(128)} %param.12) | copy-start | bytes 388
  99.4 50.6 %copy-start.5 = (s32[4,2]{0,1:T(2,128)S(1)}, s32[4,2]{0,1:T(2,128)}, u32[]{:S(2)}) copy-start(s32[4,2]{0,1:T(2,128)} %param.13) | copy-start | bytes 100
  99.4 51.2 %copy-start.9 = (s32[4]{0:T(128)S(1)}, s32[4]{0:T(128)}, u32[]{:S(2)}) copy-start(s32[4]{0:T(128)} %param.14) | copy-start | bytes 52
  142.5 56.4 %all-to-all-start.6 = ((bf16[16,2,40,640]{3,2,1,0:T(8,128)(2,1)}), bf16[16,2,40,640]{3,2,1,0:T(8,128)(2,1)}, u32[]{:S(2)}, u32[]{:S(2)}) async-start(bf16[16,2,40,640]{3,2,1,0:T(8,128)(2,1)} %get-tuple-element.3), calls=%async_computation.6 | async-start | bytes 3276800 | tf_op jit(solution)/shard_map/all_to_all | solution.py:204
  148.9 199.0 %all-gather.3.cloned.1.call-start = ((), (), s32[]{:S(2)}) async-start(), calls=%async_computation.8 | async-start | bytes 3481600 | tf_op jit(solution)/shard_map/all_gather | solution.py:210
  150.5 7.8 %copy-start.6 = (s32[4]{0:T(128)}, s32[4]{0:T(128)S(1)}, u32[]{:S(2)}) copy-start(s32[4]{0:T(128)S(1)} %get-tuple-element.19.source_ref) | copy-start | bytes 52
  198.9 44.9 %all-to-all-start.1 = ((bf16[16,2,40,640]{3,2,1,0:T(8,128)(2,1)}), bf16[16,2,40,640]{3,2,1,0:T(8,128)(2,1)}, u32[]{:S(2)}, u32[]{:S(2)}) async-start(bf16[16,2,40,640]{3,2,1,0:T(8,128)(2,1)} %bitcast.73), calls=%async_computation.1 | async-start | bytes 3276800 | tf_op jit(solution)/shard_map/all_to_all | solution.py:225
  243.7 53.3 %all-to-all-start.3 = ((bf16[16,2,40,640]{3,2,1,0:T(8,128)(2,1)}), bf16[16,2,40,640]{3,2,1,0:T(8,128)(2,1)}, u32[]{:S(2)}, u32[]{:S(2)}) async-start(bf16[16,2,40,640]{3,2,1,0:T(8,128)(2,1)} %bitcast.71), calls=%async_computation.3 | async-start | bytes 3276800 | tf_op jit(solution)/shard_map/all_to_all | solution.py:225
  248.1 99.9 %all-gather.5.cloned.1.call-start = ((), (), s32[]{:S(2)}) async-start(), calls=%async_computation.9 | async-start | bytes 3481600 | tf_op jit(solution)/shard_map/all_gather | solution.py:211
  297.1 45.8 %all-to-all-start.5 = ((bf16[16,2,40,640]{3,2,1,0:T(8,128)(2,1)}), bf16[16,2,40,640]{3,2,1,0:T(8,128)(2,1)}, u32[]{:S(2)}, u32[]{:S(2)}) async-start(bf16[16,2,40,640]{3,2,1,0:T(8,128)(2,1)} %bitcast.72), calls=%async_computation.5 | async-start | bytes 3276800 | tf_op jit(solution)/shard_map/all_to_all | solution.py:225
  305.7 42.2 %copy-start.7 = (s32[4]{0:T(128)S(1)}, s32[4]{0:T(128)}, u32[]{:S(2)}) copy-start(s32[4]{0:T(128)} %param.15) | copy-start | bytes 52
  342.9 41.9 %all-to-all-start.7 = ((bf16[16,2,40,640]{3,2,1,0:T(8,128)(2,1)}), bf16[16,2,40,640]{3,2,1,0:T(8,128)(2,1)}, u32[]{:S(2)}, u32[]{:S(2)}) async-start(bf16[16,2,40,640]{3,2,1,0:T(8,128)(2,1)} %bitcast.70), calls=%async_computation.7 | async-start | bytes 3276800 | tf_op jit(solution)/shard_map/all_to_all | solution.py:225
  354.0 4.1 copy-start.2
  384.8 7.4 %copy-start.3 = (bf16[2,640,640]{2,1,0:T(8,128)(2,1)S(1)}, bf16[2,640,640]{2,1,0:T(8,128)(2,1)}, u32[]{:S(2)}) copy-start(bf16[2,640,640]{2,1,0:T(8,128)(2,1)} %shard_map.97) | copy-start | bytes 4915204
  384.8 7.4 %copy-start.4 = (bf16[2,640,640]{2,1,0:T(8,128)(2,1)S(1)}, bf16[2,640,640]{2,1,0:T(8,128)(2,1)}, u32[]{:S(2)}) copy-start(bf16[2,640,640]{2,1,0:T(8,128)(2,1)} %shard_map.99) | copy-start | bytes 4915204
  398.8 17.4 %copy-start.1 = (f32[32,32]{1,0:T(8,128)S(1)}, f32[32,32]{1,0:T(8,128)}, u32[]{:S(2)}) copy-start(f32[32,32]{1,0:T(8,128)} %param.11) | copy-start | bytes 12292
Sparse Core Ops, SparseCore 0:
  152.0 60.7 all-gather.2
  251.2 61.1 all-gather.4

commit v2 on v0

--- a/solution.py
+++ b/solution.py
@@ -1,6 +1,10 @@
+import functools
+
 import jax
 import jax.numpy as jnp
 from jax import lax
+from jax.experimental import pallas as pl
+from jax.experimental.pallas import tpu as pltpu
 from jax.sharding import PartitionSpec as P
 
 
@@ -35,7 +39,7 @@
     return lax.all_gather(rotation_two, "ops", axis=0, tiled=True)
 
 
-def local(
+def local_general(
     normal_ops,
     rotation_one,
     rotation_two,
@@ -88,6 +92,315 @@
     return (normal_next, complementary_next)
 
 
+SUB = 8
+LIMIT = 60 * 2**20
+SHADOW = 400 * 2**20
+
+
+def greet(devices):
+    me = lax.axis_index("ops")
+    barrier = pltpu.get_barrier_semaphore()
+
+    @pl.loop(1, devices)
+    def _(step):
+        peer = lax.rem(me + step, devices)
+        pl.semaphore_signal(
+            barrier, inc=1, device_id={"ops": peer}, device_id_type=pl.DeviceIdType.MESH
+        )
+
+    pl.semaphore_wait(barrier, devices - 1)
+    return me
+
+
+def spread_kernel(
+    devices, ops_ref, weights_ref, out_ref, landed, mixed, send_sem, recv_sem, keep_sem, out_sem
+):
+    links, _, own, rows, states = landed.shape
+    me = greet(devices)
+
+    def outgoing(link, peer):
+        return pltpu.make_async_remote_copy(
+            src_ref=ops_ref.at[:, link, peer],
+            dst_ref=landed.at[link, me],
+            send_sem=send_sem.at[link, peer],
+            recv_sem=recv_sem.at[link, me],
+            device_id={"ops": peer},
+            device_id_type=pl.DeviceIdType.MESH,
+        )
+
+    def incoming(link, peer):
+        return pltpu.make_async_remote_copy(
+            src_ref=ops_ref.at[:, link, peer],
+            dst_ref=landed.at[link, peer],
+            send_sem=send_sem.at[link, peer],
+            recv_sem=recv_sem.at[link, peer],
+            device_id={"ops": peer},
+            device_id_type=pl.DeviceIdType.MESH,
+        )
+
+    def kept(link):
+        return pltpu.make_async_copy(
+            ops_ref.at[:, link, me], landed.at[link, me], keep_sem.at[link]
+        )
+
+    @pl.loop(0, links)
+    def _(link):
+        kept(link).start()
+
+        @pl.loop(1, devices)
+        def _(step):
+            outgoing(link, lax.rem(me + step, devices)).start()
+
+    @pl.loop(0, links)
+    def _(link):
+        kept(link).wait()
+
+        @pl.loop(1, devices)
+        def _(step):
+            incoming(link, lax.rem(me + step, devices)).wait_recv()
+
+        weights = weights_ref[link]
+        for start in range(0, rows, SUB):
+            piece = landed[link, :, :, start : start + SUB, :].astype(jnp.float32)
+            piece = piece.reshape(devices * own * SUB, states).astype(jnp.bfloat16)
+            total = jnp.dot(weights, piece, preferred_element_type=jnp.float32)
+            mixed[link, :, :, start : start + SUB, :] = total.reshape(
+                devices, own, SUB, states
+            ).astype(jnp.bfloat16)
+        pltpu.make_async_copy(mixed.at[link], out_ref.at[link], out_sem.at[link]).start()
+
+    @pl.loop(0, links)
+    def _(link):
+        pltpu.make_async_copy(mixed.at[link], out_ref.at[link], out_sem.at[link]).wait()
+
+        @pl.loop(1, devices)
+        def _(step):
+            outgoing(link, lax.rem(me + step, devices)).wait_send()
+
+
+def return_kernel(
+    devices,
+    couplings_ref,
+    mixed_ref,
+    ops_ref,
+    one_ref,
+    two_ref,
+    live_ref,
+    normal_ref,
+    complementary_ref,
+    landed,
+    data,
+    one,
+    two,
+    frames,
+    frames_t,
+    done,
+    send_sem,
+    recv_sem,
+    keep_sem,
+    load_sem,
+    basis_sem,
+    out_sem,
+):
+    links, own, _, rows, states = landed.shape
+    sectors = frames.shape[0]
+    blocks = data.shape[0]
+    me = greet(devices)
+
+    def copy_of(link, peer, slot):
+        return pltpu.make_async_remote_copy(
+            src_ref=mixed_ref.at[link, peer],
+            dst_ref=landed.at[link, :, slot],
+            send_sem=send_sem.at[link, peer],
+            recv_sem=recv_sem.at[link, slot],
+            device_id={"ops": peer},
+            device_id_type=pl.DeviceIdType.MESH,
+        )
+
+    def kept(link):
+        return pltpu.make_async_copy(
+            mixed_ref.at[link, me], landed.at[link, :, me], keep_sem.at[link]
+        )
+
+    @pl.loop(0, links)
+    def _(link):
+        kept(link).start()
+
+        @pl.loop(1, devices)
+        def _(step):
+            copy_of(link, lax.rem(me + step, devices), me).start()
+
+    loads = (
+        pltpu.make_async_copy(one_ref, one, basis_sem.at[0]),
+        pltpu.make_async_copy(two_ref, two, basis_sem.at[1]),
+        pltpu.make_async_copy(ops_ref, data, load_sem),
+    )
+    for load in loads:
+        load.start()
+    for load in loads:
+        load.wait()
+
+    @pl.loop(0, sectors)
+    def _(sector):
+        live = live_ref[sector]
+        frame = (
+            jnp.dot(one[sector] * live, two[sector] * live, preferred_element_type=jnp.float32)
+        )
+        frames[sector] = frame.astype(jnp.bfloat16)
+        frames_t[sector] = frame.T.astype(jnp.bfloat16)
+
+    def turn(block, link):
+        half_turn = jnp.dot(
+            block, frames[couplings_ref[link, 0]], preferred_element_type=jnp.float32
+        )
+        return jnp.dot(
+            frames_t[couplings_ref[link, 1]],
+            half_turn.astype(jnp.bfloat16),
+            preferred_element_type=jnp.float32,
+        ).astype(jnp.bfloat16)
+
+    @pl.loop(0, blocks)
+    def _(block):
+        done[0, block] = turn(data[block], lax.rem(block, links))
+        pltpu.make_async_copy(done.at[0, block], normal_ref.at[block], out_sem.at[0, block]).start()
+
+    @pl.loop(0, links)
+    def _(link):
+        kept(link).wait()
+
+        @pl.loop(1, devices)
+        def _(step):
+            peer = lax.rem(me + step, devices)
+            copy_of(link, peer, peer).wait_recv()
+
+        @pl.loop(0, own)
+        def _(place):
+            block = place * links + link
+            piece = landed[link, place].astype(jnp.float32).reshape(states, states)
+            done[1, block] = turn(piece.astype(jnp.bfloat16), link)
+            pltpu.make_async_copy(
+                done.at[1, block], complementary_ref.at[block], out_sem.at[1, block]
+            ).start()
+
+    @pl.loop(0, blocks)
+    def _(block):
+        pltpu.make_async_copy(done.at[0, block], normal_ref.at[block], out_sem.at[0, block]).wait()
+        pltpu.make_async_copy(
+            done.at[1, block], complementary_ref.at[block], out_sem.at[1, block]
+        ).wait()
+
+    @pl.loop(0, links)
+    def _(link):
+        @pl.loop(1, devices)
+        def _(step):
+            copy_of(link, lax.rem(me + step, devices), me).wait_send()
+
+
+def local(
+    normal_ops,
+    rotation_one,
+    rotation_two,
+    integrals,
+    orbital_map,
+    couplings,
+    particles,
+    state_counts,
+):
+    own_blocks, states, _ = normal_ops.shape
+    orbits = integrals.shape[0]
+    links = couplings.shape[0]
+    sectors = state_counts.shape[0]
+    devices = lax.axis_size("ops")
+    own = own_blocks // links
+    if own * links != own_blocks or states % (devices * SUB):
+        return local_general(
+            normal_ops,
+            rotation_one,
+            rotation_two,
+            integrals,
+            orbital_map,
+            couplings,
+            particles,
+            state_counts,
+        )
+    rows = states // devices
+    source, target = couplings[:, 0], couplings[:, 1]
+    chosen = (orbital_map[:, None] == jnp.arange(orbits, dtype=jnp.int32)[None, :]).astype(
+        jnp.float32
+    )
+    weights = jnp.dot(integrals, chosen.T, precision=lax.Precision.HIGHEST)
+    parity = (1 - 2 * (select_entries(particles, source) % 2)).astype(jnp.float32)
+    eye = jnp.eye(SUB, dtype=jnp.float32)
+    spread_weights = (weights[:, None, :, None] * eye[None, :, None, :]).reshape(
+        orbits * SUB, orbits * SUB
+    )
+    ops_pieces = normal_ops.reshape(own, links, devices, rows, states)
+    link_weights = (spread_weights[None] * parity[:, None, None]).astype(jnp.bfloat16)
+    live = (
+        jnp.arange(states, dtype=jnp.int32)[None, :] < state_counts[:, None]
+    ).astype(jnp.bfloat16)[:, None, :]
+    anywhere = pl.BlockSpec(memory_space=pl.ANY)
+    vmem = pl.BlockSpec(memory_space=pltpu.VMEM)
+    smem = pl.BlockSpec(memory_space=pltpu.SMEM)
+    dma = pltpu.SemaphoreType.DMA
+    basis_one = lax.all_gather(rotation_one, "ops", axis=0, tiled=True)
+    basis_two = lax.all_gather(rotation_two, "ops", axis=0, tiled=True)
+    mixed = pl.pallas_call(
+        functools.partial(spread_kernel, devices),
+        out_shape=jax.ShapeDtypeStruct((links, devices, own, rows, states), jnp.bfloat16),
+        in_specs=[anywhere, vmem],
+        out_specs=anywhere,
+        scratch_shapes=[
+            pltpu.VMEM((links, devices, own, rows, states), jnp.bfloat16),
+            pltpu.VMEM((links, devices, own, rows, states), jnp.bfloat16),
+            dma((links, devices)),
+            dma((links, devices)),
+            dma((links,)),
+            dma((links,)),
+        ],
+        compiler_params=pltpu.CompilerParams(
+            collective_id=0, has_side_effects=True, vmem_limit_bytes=LIMIT
+        ),
+        cost_estimate=pl.CostEstimate(flops=0, bytes_accessed=SHADOW, transcendentals=0),
+    )(ops_pieces, link_weights)
+    whole = (own_blocks, states, states)
+    return pl.pallas_call(
+        functools.partial(return_kernel, devices),
+        out_shape=(
+            jax.ShapeDtypeStruct(whole, jnp.bfloat16),
+            jax.ShapeDtypeStruct(whole, jnp.bfloat16),
+        ),
+        in_specs=[smem, anywhere, anywhere, anywhere, anywhere, vmem],
+        out_specs=(anywhere, anywhere),
+        scratch_shapes=[
+            pltpu.VMEM((links, own, devices, rows, states), jnp.bfloat16),
+            pltpu.VMEM(whole, jnp.bfloat16),
+            pltpu.VMEM((sectors, states, states), jnp.bfloat16),
+            pltpu.VMEM((sectors, states, states), jnp.bfloat16),
+            pltpu.VMEM((sectors, states, states), jnp.bfloat16),
+            pltpu.VMEM((sectors, states, states), jnp.bfloat16),
+            pltpu.VMEM((2,) + whole, jnp.bfloat16),
+            dma((links, devices)),
+            dma((links, devices)),
+            dma((links,)),
+            dma,
+            dma((2,)),
+            dma((2, own_blocks)),
+        ],
+        compiler_params=pltpu.CompilerParams(
+            collective_id=1, has_side_effects=True, vmem_limit_bytes=LIMIT
+        ),
+        cost_estimate=pl.CostEstimate(flops=0, bytes_accessed=SHADOW, transcendentals=0),
+    )(
+        couplings,
+        mixed,
+        normal_ops,
+        basis_one.reshape(sectors, states, states),
+        basis_two.reshape(sectors, states, states),
+        live,
+    )
+
+
 def solution(mesh):
     placed = (
         P(("groups", "ops"), None, None),

time: 748 us -> 375 us (0.50); the launches traced: 738 us -> 375 us
  Pallas kernels: 0 us -> 339 us
  waiting for transfers between devices: 319 us -> 1.38 us
  local copies, waits for them, and re-layouts: 157 us -> 14.7 us
  matrix products: 100 us -> 0.84 us
  loops' own time: 94.5 us -> 0 us
  other arithmetic: 42.3 us -> 4.48 us
  starting transfers between devices: 10.7 us -> 0.08 us
    pallas_call x0 -> x2, Pallas kernels: none -> 339 us  [the longest x1 187 us: local(): pl.pallas_call(functools.partial(spread_kernel, devices), out_shape=jax.S...]
    all_to_all x2 -> x0, waiting for transfers between devices: 143 us -> none  [the longest x1 143 us: local(): lax.all_to_all(spread, 'ops', split_axis=1, concat_axis=0, tiled=True)]
    all_gather x1, waiting for transfers between devices: 128 us -> 0.01 us  [local(): basis_two = lax.all_gather(rotation_two, 'ops', axis=0, tiled=True)]
    dot_general x26 -> x1, matrix products: 100 us -> 0.84 us  [local(): weights = jnp.dot(integrals, chosen.T, precision=lax.Precision.HIGHEST)]
    another operation x3 -> x0, loops' own time: 94.5 us -> none  [rotate(): return lax.map(single, (blocks, source, target))]
    reshape x6 -> x0, local copies, waits for them, and re-layouts: 58.2 us -> none  [the longest x2 22 us: local(): regrouped = lax.all_to_all((mixture * parity[None, :, None]).astype(jnp.b...]
    all_gather x1, waiting for transfers between devices: 47.5 us -> 0.01 us  [local(): basis_one = lax.all_gather(rotation_one, 'ops', axis=0, tiled=True)]
    reshape x1 -> x0, other arithmetic: 41.2 us -> none  [local(): regrouped = lax.all_to_all((mixture * parity[None, :, None]).astype(jnp.b...]
  transfers between devices with their start and end apart: 4 -> 2, of which waited for: 3 -> 0; matrix products, arithmetic and copies ran while one was open for 6% -> 3% of each run, Pallas kernels for 0% -> 50%
where the time goes in v2:
time: 375 us
  Pallas kernels  339 us (90%)
  local copies, waits for them, and re-layouts  14.7 us (4%)
  between operations  14.1 us (4%)
  other arithmetic  4.48 us (1%)
    pallas_call x1, Pallas kernels, local(): pl.pallas_call(functools.partial(spread_kernel, devices), out_shape=jax.S...  187 us
    pallas_call x1, Pallas kernels, local(): pl.pallas_call(functools.partial(return_kernel, devices), out_shape=(jax....  152 us
    unnamed x13, local copies, waits for them, and re-layouts  10.6 us
  transfers between devices with their start and end apart: 2, of which 0 were waited for; matrix products, arithmetic and copies ran while one was open for 3% of the time, Pallas kernels for 50%

profile of v2, /device:TPU:11, one launch (start us, length us, event | category | flops | bytes accessed | tf_op | source)
XLA Modules:
  0.0 374.8 jit_solution(16209988692401685408)
XLA Ops:
  7.2 0.0 copy-start
  7.2 0.0 copy-start.2
  7.2 0.0 copy-start.4
  7.2 0.0 all-gather.3.cloned.1.call-start
  7.2 0.7 all-gather.3.cloned.1.call-update
  7.9 0.0 all-gather.5.cloned.1.call-start
  8.0 0.7 all-gather.5.cloned.1.call-update
  8.7 1.3 copy.15.couplings_ref
  10.0 0.0 copy-done
  10.0 0.8 convolution_bitcast_fusion
  10.9 0.1 copy.14
  10.9 2.6 broadcast_multiply_fusion
  13.6 4.0 %mul.43 = f32[256,256]{1,0:T(8,128)S(1)} reshape(f32[32,8,32,8]{3,2,1,0:T(8,128)} %broadcast_multiply_fusion) | data formatting | bytes 524288 | tf_op jit(solution)/shard_map/mul | solution.py:334
  17.6 0.0 copy-done.2
  17.6 0.0 copy-done.4
  17.6 0.2 select_reduce_fusion
  17.8 1.0 multiply_convert_fusion.weights_ref
  18.8 0.0 copy-start.3
  18.8 187.4 %shard_map.95.mixed_ref = bf16[4,16,2,40,640]{4,3,2,1,0:T(8,128)(2,1)} custom-call(bf16[2,4,16,40,640]{4,3,2,1,0:T(8,128)(2,1)} %bitcast.10, bf16[4,256,256]{2,1,0:T(8,128)(2,1)} %multiply_convert_fusion.weights_ref), custom_call_target="tpu_custom_call" | custom-call | bytes 419430400 | tf_op jit(solution)/shard_map/pallas_call | solution.py:348
  206.2 0.0 copy-done.3
  206.2 0.7 compare_convert_fusion.live_ref
  206.9 0.0 all-gather.3.cloned.1.call-done
  206.9 0.0 all-gather.5.cloned.1.call-done
  206.9 151.7 %shard_map.96 = (bf16[8,640,640]{2,1,0:T(8,128)(2,1)}, bf16[8,640,640]{2,1,0:T(8,128)(2,1)}) custom-call(s32[4,2]{1,0:T(4,128)} %copy.15.couplings_ref, bf16[4,16,2,40,640]{4,3,2,1,0:T(8,128)(2,1)} %shard_map.95.mixed_ref, bf16[8,640,640]{2,1,0:T(8,128)(2,1)} %ops_ref.1, bf16[4,640,640]{2,1,0:T(8,128)(2,1)} %bitcast.11, bf16[4,640,640]{2,1,0:T(8,128)(2,1)} %bitcast.12, ...), custom_call_target="tpu_custom_call" | custom-call | bytes 419430400 | tf_op jit(solution)/shard_map/pallas_call | solution.py:367
  358.6 0.0 copy-start.1
  358.6 6.5 %copy.18 = bf16[8,640,640]{2,1,0:T(8,128)(2,1)} copy(bf16[8,640,640]{2,1,0:T(8,128)(2,1)} %get-tuple-element.4) | data formatting | bytes 13107200
  365.1 0.0 copy-done.1
  365.1 2.8 copy.19
  (3 shorter events, 0.0 us)
Async XLA Ops:
  7.2 2.9 copy-start
  7.2 10.4 %copy-start.2 = (s32[4,2]{0,1:T(2,128)S(1)}, s32[4,2]{0,1:T(2,128)}, u32[]{:S(2)}) copy-start(s32[4,2]{0,1:T(2,128)} %param.13) | copy-start | bytes 100
  7.2 10.4 %copy-start.4 = (s32[4]{0:T(128)S(1)}, s32[4]{0:T(128)}, u32[]{:S(2)}) copy-start(s32[4]{0:T(128)} %param.14) | copy-start | bytes 52
  7.2 199.7 %all-gather.3.cloned.1.call-start = ((), (), s32[]{:S(2)}) async-start(), calls=%async_computation | async-start | bytes 3481600 | tf_op jit(solution)/shard_map/all_gather | solution.py:346
  7.9 199.0 %all-gather.5.cloned.1.call-start = ((), (), s32[]{:S(2)}) async-start(), calls=%async_computation.1 | async-start | bytes 3481600 | tf_op jit(solution)/shard_map/all_gather | solution.py:347
  18.8 187.4 %copy-start.3 = (s32[4]{0:T(128)S(1)}, s32[4]{0:T(128)}, u32[]{:S(2)}) copy-start(s32[4]{0:T(128)} %param.15) | copy-start | bytes 52
  358.6 6.5 %copy-start.1 = (bf16[8,640,640]{2,1,0:T(8,128)(2,1)S(1)}, bf16[8,640,640]{2,1,0:T(8,128)(2,1)}, u32[]{:S(2)}) copy-start(bf16[8,640,640]{2,1,0:T(8,128)(2,1)} %get-tuple-element.5) | copy-start | bytes 19660804
Sparse Core Ops, SparseCore 0:
  10.3 86.7 all-gather.2
  99.4 76.2 all-gather.4

commit v3 on v0

--- a/solution.py
+++ b/solution.py
@@ -1,6 +1,11 @@
+import functools
+
 import jax
 import jax.numpy as jnp
+import numpy as np
 from jax import lax
+from jax.experimental import pallas as pl
+from jax.experimental.pallas import tpu as pltpu
 from jax.sharding import PartitionSpec as P
 
 
@@ -35,7 +40,7 @@
     return lax.all_gather(rotation_two, "ops", axis=0, tiled=True)
 
 
-def local(
+def local_general(
     normal_ops,
     rotation_one,
     rotation_two,
@@ -88,6 +93,404 @@
     return (normal_next, complementary_next)
 
 
+SUB = 8
+LIMIT = 62 * 2**20
+
+
+def greet(devices):
+    me = lax.axis_index("ops")
+    barrier = pltpu.get_barrier_semaphore()
+
+    @pl.loop(1, devices)
+    def _(step):
+        peer = lax.rem(me + step, devices)
+        pl.semaphore_signal(
+            barrier, inc=1, device_id={"ops": peer}, device_id_type=pl.DeviceIdType.MESH
+        )
+
+    pl.semaphore_wait(barrier, devices - 1)
+    return me
+
+
+def send(source, place, send_sem, recv_sem, peer):
+    return pltpu.make_async_remote_copy(
+        src_ref=source,
+        dst_ref=place,
+        send_sem=send_sem,
+        recv_sem=recv_sem,
+        device_id={"ops": peer},
+        device_id_type=pl.DeviceIdType.MESH,
+    )
+
+
+def sweep_kernel(
+    devices,
+    couplings_ref,
+    parity_ref,
+    integrals_ref,
+    chosen_ref,
+    widen_ref,
+    same_ref,
+    live_ref,
+    pieces_ref,
+    ops_ref,
+    one_ref,
+    two_ref,
+    normal_ref,
+    complementary_ref,
+    entries,
+    stage,
+    landed,
+    data,
+    one,
+    two,
+    own_frame,
+    strips,
+    frames,
+    frames_t,
+    done,
+    send_one,
+    recv_one,
+    send_two,
+    recv_two,
+    send_basis,
+    recv_basis,
+    send_strip,
+    recv_strip,
+    send_relay,
+    recv_relay,
+    keep_one,
+    keep_two,
+    load_sem,
+    stage_sem,
+    out_sem,
+):
+    links, own, _, rows, states = landed.shape
+    sectors = frames.shape[0]
+    blocks = data.shape[0]
+    team = devices // sectors
+    me = greet(devices)
+    sector, rank = lax.div(me, team), lax.rem(me, team)
+
+    def basis_copy(peer_rank, slot):
+        return send(
+            two_ref,
+            two.at[slot],
+            send_basis.at[peer_rank],
+            recv_basis.at[slot],
+            sector * team + peer_rank,
+        )
+
+    def strip_copy(peer_sector, slot):
+        return send(
+            strips.at[slot * team + rank],
+            strips.at[slot * team + rank],
+            send_strip.at[peer_sector],
+            recv_strip.at[slot],
+            peer_sector * team + rank,
+        )
+
+    def relay_copy(peer_rank, of_sector, of_rank):
+        return send(
+            strips.at[of_sector * team + of_rank],
+            strips.at[of_sector * team + of_rank],
+            send_relay.at[peer_rank, of_sector],
+            recv_relay.at[of_rank, of_sector],
+            sector * team + peer_rank,
+        )
+
+    def entry_copy(link, peer, slot):
+        return send(
+            pieces_ref.at[:, link, peer],
+            entries.at[link, slot],
+            send_one.at[link, peer],
+            recv_one.at[link, slot],
+            peer,
+        )
+
+    def return_copy(link, peer, slot):
+        return send(
+            entries.at[link, peer],
+            landed.at[link, :, slot],
+            send_two.at[link, peer],
+            recv_two.at[link, slot],
+            peer,
+        )
+
+    def kept_one(link):
+        return pltpu.make_async_copy(
+            pieces_ref.at[:, link, me], entries.at[link, me], keep_one.at[link]
+        )
+
+    def kept_two(link):
+        return pltpu.make_async_copy(
+            entries.at[link, me], landed.at[link, :, me], keep_two.at[link]
+        )
+
+    @pl.loop(1, team)
+    def _(step):
+        basis_copy(lax.rem(rank + step, team), rank).start()
+
+    @pl.loop(0, links)
+    def _(link):
+        kept_one(link).start()
+
+        @pl.loop(1, devices)
+        def _(step):
+            entry_copy(link, lax.rem(me + step, devices), me).start()
+
+    load_one = pltpu.make_async_copy(one_ref, one, load_sem.at[0])
+    load_two = pltpu.make_async_copy(two_ref, two.at[rank], load_sem.at[1])
+    load_data = pltpu.make_async_copy(ops_ref, data, load_sem.at[2])
+    load_one.start()
+    load_two.start()
+    load_data.start()
+
+    weights = jnp.dot(widen_ref[...], integrals_ref[...], preferred_element_type=jnp.float32)
+    weights = jnp.dot(
+        weights.astype(jnp.bfloat16), chosen_ref[...], preferred_element_type=jnp.float32
+    )
+    weights = weights * same_ref[...]
+
+    load_one.wait()
+    load_two.wait()
+
+    @pl.loop(1, team)
+    def _(step):
+        peer_rank = lax.rem(rank + step, team)
+        basis_copy(peer_rank, peer_rank).wait_recv()
+
+    live = live_ref[sector]
+    own_frame[...] = jnp.dot(
+        one[...] * live,
+        two[...].reshape(states, states) * live,
+        preferred_element_type=jnp.float32,
+    ).astype(jnp.bfloat16)
+    own_strip = pltpu.make_async_copy(own_frame, strips.at[me], load_sem.at[3])
+    own_strip.start()
+    own_strip.wait()
+
+    @pl.loop(1, sectors)
+    def _(step):
+        strip_copy(lax.rem(sector + step, sectors), sector).start()
+
+    @pl.loop(0, links)
+    def _(link):
+        kept_one(link).wait()
+
+        @pl.loop(1, devices)
+        def _(step):
+            peer = lax.rem(me + step, devices)
+            entry_copy(link, peer, peer).wait_recv()
+
+        signed = (weights * parity_ref[link]).astype(jnp.bfloat16)
+        for start in range(0, rows, SUB):
+            piece = entries[link, :, :, start : start + SUB, :].astype(jnp.float32)
+            piece = piece.reshape(devices * own * SUB, states).astype(jnp.bfloat16)
+            total = jnp.dot(signed, piece, preferred_element_type=jnp.float32)
+            stage[:, :, start : start + SUB, :] = total.reshape(devices, own, SUB, states).astype(
+                jnp.bfloat16
+            )
+        moved = pltpu.make_async_copy(stage, entries.at[link], stage_sem)
+        moved.start()
+        moved.wait()
+        kept_two(link).start()
+
+        @pl.loop(1, devices)
+        def _(step):
+            return_copy(link, lax.rem(me + step, devices), me).start()
+
+    @pl.loop(1, sectors)
+    def _(step):
+        peer_sector = lax.rem(sector + step, sectors)
+        strip_copy(peer_sector, peer_sector).wait_recv()
+
+    @pl.loop(1, team)
+    def _(step):
+        peer_rank = lax.rem(rank + step, team)
+
+        @pl.loop(0, sectors)
+        def _(of_sector):
+            relay_copy(peer_rank, of_sector, rank).start()
+
+    load_data.wait()
+
+    @pl.loop(1, team)
+    def _(step):
+        peer_rank = lax.rem(rank + step, team)
+
+        @pl.loop(0, sectors)
+        def _(of_sector):
+            relay_copy(peer_rank, of_sector, peer_rank).wait_recv()
+
+    @pl.loop(0, sectors)
+    def _(index):
+        frame = strips[pl.ds(index * team, team)].reshape(states, states)
+        frames[index] = frame
+        frames_t[index] = frame.astype(jnp.float32).T.astype(jnp.bfloat16)
+
+    def turn(block, link):
+        half_turn = jnp.dot(
+            block, frames[couplings_ref[link, 0]], preferred_element_type=jnp.float32
+        )
+        return jnp.dot(
+            frames_t[couplings_ref[link, 1]],
+            half_turn.astype(jnp.bfloat16),
+            preferred_element_type=jnp.float32,
+        ).astype(jnp.bfloat16)
+
+    def write(which, target, block):
+        return pltpu.make_async_copy(
+            done.at[which, block], target.at[block], out_sem.at[which, block]
+        )
+
+    @pl.loop(0, blocks)
+    def _(block):
+        done[0, block] = turn(data[block], lax.rem(block, links))
+        write(0, normal_ref, block).start()
+
+    @pl.loop(0, links)
+    def _(link):
+        kept_two(link).wait()
+
+        @pl.loop(1, devices)
+        def _(step):
+            peer = lax.rem(me + step, devices)
+            return_copy(link, peer, peer).wait_recv()
+
+        @pl.loop(0, own)
+        def _(place):
+            block = place * links + link
+            piece = landed[link, place].astype(jnp.float32).reshape(states, states)
+            done[1, block] = turn(piece.astype(jnp.bfloat16), link)
+            write(1, complementary_ref, block).start()
+
+    @pl.loop(1, team)
+    def _(step):
+        peer_rank = lax.rem(rank + step, team)
+        basis_copy(peer_rank, rank).wait_send()
+
+        @pl.loop(0, sectors)
+        def _(of_sector):
+            relay_copy(peer_rank, of_sector, rank).wait_send()
+
+    @pl.loop(1, sectors)
+    def _(step):
+        strip_copy(lax.rem(sector + step, sectors), sector).wait_send()
+
+    @pl.loop(0, links)
+    def _(link):
+        @pl.loop(1, devices)
+        def _(step):
+            peer = lax.rem(me + step, devices)
+            entry_copy(link, peer, me).wait_send()
+            return_copy(link, peer, me).wait_send()
+
+    @pl.loop(0, blocks)
+    def _(block):
+        write(0, normal_ref, block).wait()
+        write(1, complementary_ref, block).wait()
+
+
+def local(
+    normal_ops,
+    rotation_one,
+    rotation_two,
+    integrals,
+    orbital_map,
+    couplings,
+    particles,
+    state_counts,
+):
+    own_blocks, states, _ = normal_ops.shape
+    orbits = integrals.shape[0]
+    links = couplings.shape[0]
+    sectors = state_counts.shape[0]
+    devices = lax.axis_size("ops")
+    own = own_blocks // links
+    if own * links != own_blocks or states % (devices * SUB) or devices % sectors:
+        return local_general(
+            normal_ops,
+            rotation_one,
+            rotation_two,
+            integrals,
+            orbital_map,
+            couplings,
+            particles,
+            state_counts,
+        )
+    rows = states // devices
+    team = devices // sectors
+    parity = (1 - 2 * (select_entries(particles, couplings[:, 0]) % 2)).astype(jnp.float32)
+    wide = np.arange(orbits * SUB)
+    widen = jnp.asarray(wide[:, None] // SUB == np.arange(orbits)[None, :], jnp.bfloat16)
+    same = jnp.asarray(wide[:, None] % SUB == wide[None, :] % SUB, jnp.float32)
+    chosen = (
+        jnp.arange(orbits, dtype=jnp.int32)[:, None] == jnp.repeat(orbital_map, SUB)[None, :]
+    ).astype(jnp.bfloat16)
+    live = (
+        jnp.arange(states, dtype=jnp.int32)[None, :] < state_counts[:, None]
+    ).astype(jnp.bfloat16)[:, None, :]
+    anywhere = pl.BlockSpec(memory_space=pl.ANY)
+    vmem = pl.BlockSpec(memory_space=pltpu.VMEM)
+    smem = pl.BlockSpec(memory_space=pltpu.SMEM)
+    dma = pltpu.SemaphoreType.DMA
+    whole = (own_blocks, states, states)
+    strip = rotation_one.shape
+    return pl.pallas_call(
+        functools.partial(sweep_kernel, devices),
+        out_shape=(
+            jax.ShapeDtypeStruct(whole, jnp.bfloat16),
+            jax.ShapeDtypeStruct(whole, jnp.bfloat16),
+        ),
+        in_specs=[smem, smem, vmem, vmem, vmem, vmem, vmem] + [anywhere] * 4,
+        out_specs=(anywhere, anywhere),
+        scratch_shapes=[
+            pltpu.VMEM((links, devices, own, rows, states), jnp.bfloat16),
+            pltpu.VMEM((devices, own, rows, states), jnp.bfloat16),
+            pltpu.VMEM((links, own, devices, rows, states), jnp.bfloat16),
+            pltpu.VMEM(whole, jnp.bfloat16),
+            pltpu.VMEM(strip, jnp.bfloat16),
+            pltpu.VMEM((team,) + strip, jnp.bfloat16),
+            pltpu.VMEM(strip, jnp.bfloat16),
+            pltpu.VMEM((devices,) + strip, jnp.bfloat16),
+            pltpu.VMEM((sectors, states, states), jnp.bfloat16),
+            pltpu.VMEM((sectors, states, states), jnp.bfloat16),
+            pltpu.VMEM((2,) + whole, jnp.bfloat16),
+            dma((links, devices)),
+            dma((links, devices)),
+            dma((links, devices)),
+            dma((links, devices)),
+            dma((team,)),
+            dma((team,)),
+            dma((sectors,)),
+            dma((sectors,)),
+            dma((team, sectors)),
+            dma((team, sectors)),
+            dma((links,)),
+            dma((links,)),
+            dma((4,)),
+            dma,
+            dma((2, own_blocks)),
+        ],
+        compiler_params=pltpu.CompilerParams(
+            collective_id=0, has_side_effects=True, vmem_limit_bytes=LIMIT
+        ),
+    )(
+        couplings,
+        parity,
+        integrals.astype(jnp.bfloat16),
+        chosen,
+        widen,
+        same,
+        live,
+        normal_ops.reshape(own, links, devices, rows, states),
+        normal_ops,
+        rotation_one,
+        rotation_two,
+    )
+
+
 def solution(mesh):
     placed = (
         P(("groups", "ops"), None, None),

time: 748 us -> 334 us (0.45)
  waiting for transfers between devices: 319 us -> 0 us
  Pallas kernels: 0 us -> 313 us
  local copies, waits for them, and re-layouts: 157 us -> 12.1 us
  matrix products: 100 us -> 0 us
  loops' own time: 94.5 us -> 0 us
  other arithmetic: 42.3 us -> 4.63 us
  between operations: 14.1 us -> 0.65 us
  starting transfers between devices: 10.7 us -> 0 us
    pallas_call x0 -> x1, Pallas kernels: none -> 313 us  [local(): pl.pallas_call(functools.partial(sweep_kernel, devices), out_shape=(jax.S...]
    all_gather x2 -> x0, waiting for transfers between devices: 175 us -> none  [the longest x1 128 us: fetch_second(): return lax.all_gather(rotation_two, 'ops', axis=0, tiled=True)]
    all_to_all x2 -> x0, waiting for transfers between devices: 143 us -> none  [the longest x1 143 us: local(): lax.all_to_all(spread, 'ops', split_axis=1, concat_axis=0, tiled=True)]
    dot_general x26 -> x0, matrix products: 100 us -> none  [the longest x24 90.2 us: single(): lax.dot_general(frame_out, half_turn, (((0,), (0,)), ((), ())), preferred...]
    another operation x3 -> x0, loops' own time: 94.5 us -> none  [rotate(): return lax.map(single, (blocks, source, target))]
    reshape x6 -> x0, local copies, waits for them, and re-layouts: 58.2 us -> none  [the longest x2 22 us: local(): regrouped = lax.all_to_all((mixture * parity[None, :, None]).astype(jnp.b...]
    reshape x1 -> x0, other arithmetic: 41.2 us -> none  [local(): regrouped = lax.all_to_all((mixture * parity[None, :, None]).astype(jnp.b...]
    dynamic_slice x72 -> x0, local copies, waits for them, and re-layouts: 30.8 us -> none  [the longest x48 30.2 us: rotate(): return lax.map(single, (blocks, source, target))]
  transfers between devices with their start and end apart: 4 -> 0, of which waited for: 3 -> 0; matrix products, arithmetic and copies ran while one was open for 6% -> 0% of each run, Pallas kernels for 0% -> 0%
where the time goes in v3:
time: 334 us; the launch traced here: 330 us
  Pallas kernels  313 us (94%)
  local copies, waits for them, and re-layouts  12.1 us (4%)
  other arithmetic  4.63 us (1%)
    pallas_call x1, Pallas kernels, local(): pl.pallas_call(functools.partial(sweep_kernel, devices), out_shape=(jax.S...  313 us
    unnamed x5, local copies, waits for them, and re-layouts  10.6 us

profile of v3, /device:TPU:11, one launch (start us, length us, event | category | flops | bytes accessed | tf_op | source)
XLA Modules:
  0.0 330.1 jit_solution(5184403791423389583)
XLA Ops:
  0.6 0.7 slice_bitcast_fusion
  1.3 0.8 select_reduce_fusion
  2.1 0.5 fusion.3.parity_ref
  2.7 1.4 copy.14.couplings_ref
  4.0 1.3 convert_element_type.20.integrals_ref
  5.3 1.3 compare_convert_fusion.live_ref
  6.7 0.7 broadcast_in_dim.23
  7.4 0.1 eq.37
  7.5 0.6 fusion.chosen_ref
  8.1 312.7 %shard_map.113 = (bf16[8,640,640]{2,1,0:T(8,128)(2,1)}, bf16[8,640,640]{2,1,0:T(8,128)(2,1)}) custom-call(s32[4,2]{1,0:T(4,128)} %copy.14.couplings_ref, f32[4]{0:T(128)} %fusion.3.parity_ref, bf16[32,32]{1,0:T(8,128)(2,1)} %convert_element_type.20.integrals_ref, bf16[32,256]{1,0:T(8,128)(2,1)} %fusion.chosen_ref, bf16[256,32]{1,0:T(8,128)(2,1)} %constant.22.clone.widen_ref, ...), custom_call_target="tpu_custom_call" | custom-call | tf_op jit(solution)/shard_map/pallas_call | solution.py:440
  320.8 0.0 copy-start
  320.8 6.5 %copy.17 = bf16[8,640,640]{2,1,0:T(8,128)(2,1)} copy(bf16[8,640,640]{2,1,0:T(8,128)(2,1)} %get-tuple-element.4) | data formatting | bytes 13107200
  327.3 0.0 copy-done
  327.3 2.8 copy.18
Async XLA Ops:
  320.8 6.5 %copy-start = (bf16[8,640,640]{2,1,0:T(8,128)(2,1)S(1)}, bf16[8,640,640]{2,1,0:T(8,128)(2,1)}, u32[]{:S(2)}) copy-start(bf16[8,640,640]{2,1,0:T(8,128)(2,1)} %get-tuple-element.5) | copy-start | bytes 19660804

commit v4 on v3

--- a/solution.py
+++ b/solution.py
@@ -126,12 +126,12 @@
 def sweep_kernel(
     devices,
     couplings_ref,
-    parity_ref,
+    particles_ref,
+    counts_ref,
+    orbital_ref,
     integrals_ref,
-    chosen_ref,
     widen_ref,
     same_ref,
-    live_ref,
     pieces_ref,
     ops_ref,
     one_ref,
@@ -149,6 +149,7 @@
     frames,
     frames_t,
     done,
+    chosen,
     send_one,
     recv_one,
     send_two,
@@ -181,14 +182,23 @@
             sector * team + peer_rank,
         )
 
+    half = sectors // 2
+    across = lax.rem(sector + half, sectors)
+
     def strip_copy(peer_sector, slot):
         return send(
             strips.at[slot * team + rank],
             strips.at[slot * team + rank],
-            send_strip.at[peer_sector],
+            send_strip.at[peer_sector, slot],
             recv_strip.at[slot],
             peer_sector * team + rank,
         )
+
+    def neighbour(step):
+        return lax.div(sector, half) * half + lax.rem(sector + step, half)
+
+    def crossed(peer_sector):
+        return lax.rem(peer_sector + half, sectors)
 
     def relay_copy(peer_rank, of_sector, of_rank):
         return send(
@@ -231,13 +241,14 @@
     def _(step):
         basis_copy(lax.rem(rank + step, team), rank).start()
 
-    @pl.loop(0, links)
-    def _(link):
+    def send_entries(link):
         kept_one(link).start()
 
         @pl.loop(1, devices)
         def _(step):
             entry_copy(link, lax.rem(me + step, devices), me).start()
+
+    send_entries(0)
 
     load_one = pltpu.make_async_copy(one_ref, one, load_sem.at[0])
     load_two = pltpu.make_async_copy(two_ref, two.at[rank], load_sem.at[1])
@@ -246,12 +257,6 @@
     load_two.start()
     load_data.start()
 
-    weights = jnp.dot(widen_ref[...], integrals_ref[...], preferred_element_type=jnp.float32)
-    weights = jnp.dot(
-        weights.astype(jnp.bfloat16), chosen_ref[...], preferred_element_type=jnp.float32
-    )
-    weights = weights * same_ref[...]
-
     load_one.wait()
     load_two.wait()
 
@@ -260,7 +265,8 @@
         peer_rank = lax.rem(rank + step, team)
         basis_copy(peer_rank, peer_rank).wait_recv()
 
-    live = live_ref[sector]
+    columns = lax.broadcasted_iota(jnp.int32, (1, states), 1)
+    live = (columns < counts_ref[sector]).astype(jnp.float32).astype(jnp.bfloat16)
     own_frame[...] = jnp.dot(
         one[...] * live,
         two[...].reshape(states, states) * live,
@@ -270,12 +276,34 @@
     own_strip.start()
     own_strip.wait()
 
-    @pl.loop(1, sectors)
-    def _(step):
-        strip_copy(lax.rem(sector + step, sectors), sector).start()
-
-    @pl.loop(0, links)
+    strip_copy(across, sector).start()
+
+    @pl.loop(1, links)
     def _(link):
+        send_entries(link)
+
+    orbits = integrals_ref.shape[0]
+    places = lax.broadcasted_iota(jnp.int32, (1, orbits), 1)
+    for orbital in range(orbits):
+        chosen[orbital : orbital + 1, :] = (places == orbital_ref[orbital]).astype(jnp.float32)
+    weights = lax.dot_general(
+        integrals_ref[...].astype(jnp.bfloat16),
+        chosen[...].astype(jnp.bfloat16),
+        (((1,), (1,)), ((), ())),
+        preferred_element_type=jnp.float32,
+    )
+    weights = jnp.dot(
+        widen_ref[...], weights.astype(jnp.bfloat16), preferred_element_type=jnp.float32
+    )
+    weights = lax.dot_general(
+        weights.astype(jnp.bfloat16),
+        widen_ref[...],
+        (((1,), (1,)), ((), ())),
+        preferred_element_type=jnp.float32,
+    )
+    weights = weights * same_ref[...]
+
+    def mix_link(link):
         kept_one(link).wait()
 
         @pl.loop(1, devices)
@@ -283,7 +311,8 @@
             peer = lax.rem(me + step, devices)
             entry_copy(link, peer, peer).wait_recv()
 
-        signed = (weights * parity_ref[link]).astype(jnp.bfloat16)
+        parity = (1 - 2 * lax.rem(particles_ref[couplings_ref[0, link]], 2)).astype(jnp.float32)
+        signed = (weights * parity).astype(jnp.bfloat16)
         for start in range(0, rows, SUB):
             piece = entries[link, :, :, start : start + SUB, :].astype(jnp.float32)
             piece = piece.reshape(devices * own * SUB, states).astype(jnp.bfloat16)
@@ -300,10 +329,22 @@
         def _(step):
             return_copy(link, lax.rem(me + step, devices), me).start()
 
-    @pl.loop(1, sectors)
-    def _(step):
-        peer_sector = lax.rem(sector + step, sectors)
-        strip_copy(peer_sector, peer_sector).wait_recv()
+    mix_link(0)
+    strip_copy(across, across).wait_recv()
+
+    @pl.loop(1, half)
+    def _(step):
+        strip_copy(neighbour(step), sector).start()
+        strip_copy(neighbour(step), across).start()
+
+    @pl.loop(1, min(2, links))
+    def _(link):
+        mix_link(link)
+
+    @pl.loop(1, half)
+    def _(step):
+        strip_copy(neighbour(step), neighbour(step)).wait_recv()
+        strip_copy(neighbour(step), crossed(neighbour(step))).wait_recv()
 
     @pl.loop(1, team)
     def _(step):
@@ -312,6 +353,10 @@
         @pl.loop(0, sectors)
         def _(of_sector):
             relay_copy(peer_rank, of_sector, rank).start()
+
+    @pl.loop(min(2, links), links)
+    def _(link):
+        mix_link(link)
 
     load_data.wait()
 
@@ -331,10 +376,10 @@
 
     def turn(block, link):
         half_turn = jnp.dot(
-            block, frames[couplings_ref[link, 0]], preferred_element_type=jnp.float32
+            block, frames[couplings_ref[0, link]], preferred_element_type=jnp.float32
         )
         return jnp.dot(
-            frames_t[couplings_ref[link, 1]],
+            frames_t[couplings_ref[1, link]],
             half_turn.astype(jnp.bfloat16),
             preferred_element_type=jnp.float32,
         ).astype(jnp.bfloat16)
@@ -374,9 +419,12 @@
         def _(of_sector):
             relay_copy(peer_rank, of_sector, rank).wait_send()
 
-    @pl.loop(1, sectors)
-    def _(step):
-        strip_copy(lax.rem(sector + step, sectors), sector).wait_send()
+    strip_copy(across, sector).wait_send()
+
+    @pl.loop(1, half)
+    def _(step):
+        strip_copy(neighbour(step), sector).wait_send()
+        strip_copy(neighbour(step), across).wait_send()
 
     @pl.loop(0, links)
     def _(link):
@@ -408,7 +456,7 @@
     sectors = state_counts.shape[0]
     devices = lax.axis_size("ops")
     own = own_blocks // links
-    if own * links != own_blocks or states % (devices * SUB) or devices % sectors:
+    if own * links != own_blocks or states % (devices * SUB) or devices % sectors or sectors % 2:
         return local_general(
             normal_ops,
             rotation_one,
@@ -421,16 +469,9 @@
         )
     rows = states // devices
     team = devices // sectors
-    parity = (1 - 2 * (select_entries(particles, couplings[:, 0]) % 2)).astype(jnp.float32)
     wide = np.arange(orbits * SUB)
     widen = jnp.asarray(wide[:, None] // SUB == np.arange(orbits)[None, :], jnp.bfloat16)
     same = jnp.asarray(wide[:, None] % SUB == wide[None, :] % SUB, jnp.float32)
-    chosen = (
-        jnp.arange(orbits, dtype=jnp.int32)[:, None] == jnp.repeat(orbital_map, SUB)[None, :]
-    ).astype(jnp.bfloat16)
-    live = (
-        jnp.arange(states, dtype=jnp.int32)[None, :] < state_counts[:, None]
-    ).astype(jnp.bfloat16)[:, None, :]
     anywhere = pl.BlockSpec(memory_space=pl.ANY)
     vmem = pl.BlockSpec(memory_space=pltpu.VMEM)
     smem = pl.BlockSpec(memory_space=pltpu.SMEM)
@@ -443,7 +484,7 @@
             jax.ShapeDtypeStruct(whole, jnp.bfloat16),
             jax.ShapeDtypeStruct(whole, jnp.bfloat16),
         ),
-        in_specs=[smem, smem, vmem, vmem, vmem, vmem, vmem] + [anywhere] * 4,
+        in_specs=[smem] * 4 + [vmem] * 3 + [anywhere] * 4,
         out_specs=(anywhere, anywhere),
         scratch_shapes=[
             pltpu.VMEM((links, devices, own, rows, states), jnp.bfloat16),
@@ -457,13 +498,14 @@
             pltpu.VMEM((sectors, states, states), jnp.bfloat16),
             pltpu.VMEM((sectors, states, states), jnp.bfloat16),
             pltpu.VMEM((2,) + whole, jnp.bfloat16),
+            pltpu.VMEM((orbits, orbits), jnp.float32),
             dma((links, devices)),
             dma((links, devices)),
             dma((links, devices)),
             dma((links, devices)),
             dma((team,)),
             dma((team,)),
-            dma((sectors,)),
+            dma((sectors, sectors)),
             dma((sectors,)),
             dma((team, sectors)),
             dma((team, sectors)),
@@ -477,13 +519,13 @@
             collective_id=0, has_side_effects=True, vmem_limit_bytes=LIMIT
         ),
     )(
-        couplings,
-        parity,
-        integrals.astype(jnp.bfloat16),
-        chosen,
+        couplings.T,
+        particles,
+        state_counts,
+        orbital_map,
+        integrals,
         widen,
         same,
-        live,
         normal_ops.reshape(own, links, devices, rows, states),
         normal_ops,
         rotation_one,

time: 334 us -> 314 us (0.940); the launches traced: 330 us -> 314 us
  Pallas kernels: 313 us -> 304 us
  other arithmetic: 4.63 us -> 0 us
    pallas_call x1, Pallas kernels: 313 us -> 304 us  [local(): pl.pallas_call(functools.partial(sweep_kernel, devices), out_shape=(jax.S...]
    convert_element_type x4 -> x0, other arithmetic: 3.79 us -> none  [the longest x1 1.33 us: local(): live = (jnp.arange(states, dtype=jnp.int32)[None, :] < state_counts[:, No...]
    unnamed x5 -> x4, local copies, waits for them, and re-layouts: 10.6 us -> 9.28 us
where the time goes in v4:
time: 314 us
  Pallas kernels  304 us (97%)
  local copies, waits for them, and re-layouts  9.28 us (3%)
    pallas_call x1, Pallas kernels, local(): pl.pallas_call(functools.partial(sweep_kernel, devices), out_shape=(jax.S...  304 us
    unnamed x4, local copies, waits for them, and re-layouts  9.28 us

profile of v4, /device:TPU:11, one launch (start us, length us, event | category | flops | bytes accessed | tf_op | source)
XLA Modules:
  0.0 313.8 jit_solution(13520121788837114511)
XLA Ops:
  0.6 303.9 %shard_map.113 = (bf16[8,640,640]{2,1,0:T(8,128)(2,1)}, bf16[8,640,640]{2,1,0:T(8,128)(2,1)}) custom-call(s32[2,4]{1,0:T(2,128)} %bitcast.3, s32[4]{0:T(128)} %particles_ref.1, s32[4]{0:T(128)} %counts_ref.1, s32[32]{0:T(128)} %orbital_ref.1, f32[32,32]{1,0:T(8,128)} %integrals_ref.1, bf16[256,32]{1,0:T(8,128)(2,1)} %constant.4.clone.widen_ref, ...), custom_call_target="tpu_custom_call" | custom-call | tf_op jit(solution)/shard_map/pallas_call | solution.py:481
  304.5 0.0 copy-start
  304.5 6.5 %copy.14 = bf16[8,640,640]{2,1,0:T(8,128)(2,1)} copy(bf16[8,640,640]{2,1,0:T(8,128)(2,1)} %get-tuple-element.4) | data formatting | bytes 13107200
  311.0 0.0 copy-done
  311.0 2.8 copy.15
Async XLA Ops:
  304.5 6.5 %copy-start = (bf16[8,640,640]{2,1,0:T(8,128)(2,1)S(1)}, bf16[8,640,640]{2,1,0:T(8,128)(2,1)}, u32[]{:S(2)}) copy-start(bf16[8,640,640]{2,1,0:T(8,128)(2,1)} %get-tuple-element.5) | copy-start | bytes 19660804

commit v5 on v4

--- a/solution.py
+++ b/solution.py
@@ -138,6 +138,8 @@
     two_ref,
     normal_ref,
     complementary_ref,
+    frames_out,
+    frames_t_out,
     entries,
     stage,
     landed,
@@ -394,8 +396,14 @@
         done[0, block] = turn(data[block], lax.rem(block, links))
         write(0, normal_ref, block).start()
 
-    @pl.loop(0, links)
-    def _(link):
+    frame_copies = (
+        pltpu.make_async_copy(frames, frames_out, load_sem.at[4]),
+        pltpu.make_async_copy(frames_t, frames_t_out, load_sem.at[5]),
+    )
+    for copy in frame_copies:
+        copy.start()
+
+    def collect(link, last):
         kept_two(link).wait()
 
         @pl.loop(1, devices)
@@ -407,8 +415,17 @@
         def _(place):
             block = place * links + link
             piece = landed[link, place].astype(jnp.float32).reshape(states, states)
-            done[1, block] = turn(piece.astype(jnp.bfloat16), link)
+            piece = piece.astype(jnp.bfloat16)
+            done[1, block] = piece if last else turn(piece, link)
             write(1, complementary_ref, block).start()
+
+    @pl.loop(0, links - 1)
+    def _(link):
+        collect(link, False)
+
+    collect(links - 1, True)
+    for copy in frame_copies:
+        copy.wait()
 
     @pl.loop(1, team)
     def _(step):
@@ -438,6 +455,24 @@
     def _(block):
         write(0, normal_ref, block).wait()
         write(1, complementary_ref, block).wait()
+
+
+def finish_kernel(
+    links, ends_ref, normal_in, complementary_in, frame_in, frame_out, normal_ref, complementary_ref
+):
+    normal_ref[...] = normal_in[...]
+    last = lax.rem(pl.program_id(0), links) == links - 1
+
+    @pl.when(last)
+    def _():
+        half_turn = jnp.dot(complementary_in[0], frame_in[0], preferred_element_type=jnp.float32)
+        complementary_ref[0] = jnp.dot(
+            frame_out[0], half_turn.astype(jnp.bfloat16), preferred_element_type=jnp.float32
+        ).astype(jnp.bfloat16)
+
+    @pl.when(jnp.logical_not(last))
+    def _():
+        complementary_ref[...] = complementary_in[...]
 
 
 def local(
@@ -478,14 +513,16 @@
     dma = pltpu.SemaphoreType.DMA
     whole = (own_blocks, states, states)
     strip = rotation_one.shape
-    return pl.pallas_call(
+    swept = pl.pallas_call(
         functools.partial(sweep_kernel, devices),
         out_shape=(
             jax.ShapeDtypeStruct(whole, jnp.bfloat16),
             jax.ShapeDtypeStruct(whole, jnp.bfloat16),
+            jax.ShapeDtypeStruct((sectors, states, states), jnp.bfloat16),
+            jax.ShapeDtypeStruct((sectors, states, states), jnp.bfloat16),
         ),
         in_specs=[smem] * 4 + [vmem] * 3 + [anywhere] * 4,
-        out_specs=(anywhere, anywhere),
+        out_specs=(anywhere,) * 4,
         scratch_shapes=[
             pltpu.VMEM((links, devices, own, rows, states), jnp.bfloat16),
             pltpu.VMEM((devices, own, rows, states), jnp.bfloat16),
@@ -511,7 +548,7 @@
             dma((team, sectors)),
             dma((links,)),
             dma((links,)),
-            dma((4,)),
+            dma((6,)),
             dma,
             dma((2, own_blocks)),
         ],
@@ -531,6 +568,26 @@
         rotation_one,
         rotation_two,
     )
+    ends = couplings[links - 1]
+    block_spec = pl.BlockSpec((1, states, states), lambda b, e: (b, 0, 0))
+    return pl.pallas_call(
+        functools.partial(finish_kernel, links),
+        grid_spec=pltpu.PrefetchScalarGridSpec(
+            num_scalar_prefetch=1,
+            grid=(own_blocks,),
+            in_specs=[
+                block_spec,
+                block_spec,
+                pl.BlockSpec((1, states, states), lambda b, e: (e[0], 0, 0)),
+                pl.BlockSpec((1, states, states), lambda b, e: (e[1], 0, 0)),
+            ],
+            out_specs=(block_spec, block_spec),
+        ),
+        out_shape=(
+            jax.ShapeDtypeStruct(whole, jnp.bfloat16),
+            jax.ShapeDtypeStruct(whole, jnp.bfloat16),
+        ),
+    )(ends, *swept)
 
 
 def solution(mesh):

time: 314 us -> 319 us (1.016)
  Pallas kernels: 304 us -> 317 us
  local copies, waits for them, and re-layouts: 9.28 us -> 1.37 us
    pallas_call x0 -> x1, Pallas kernels: none -> 15.8 us  [local(): pl.pallas_call(functools.partial(finish_kernel, links), grid_spec=pltpu.P...]
    unnamed x4 -> x0, local copies, waits for them, and re-layouts: 9.28 us -> none
where the time goes in v5:
time: 319 us
  Pallas kernels  317 us (99%)
    pallas_call x1, Pallas kernels, local(): pl.pallas_call(functools.partial(sweep_kernel, devices), out_shape=(jax.S...  301 us
    pallas_call x1, Pallas kernels, local(): pl.pallas_call(functools.partial(finish_kernel, links), grid_spec=pltpu.P...  15.8 us

profile of v5, /device:TPU:11, one launch (start us, length us, event | category | flops | bytes accessed | tf_op | source)
XLA Modules:
  0.0 318.8 jit_solution(16387453125357793569)
XLA Ops:
  0.6 1.4 slice_reduce_fusion.ends_ref
  2.0 301.0 %shard_map.113 = (bf16[8,640,640]{2,1,0:T(8,128)(2,1)}, bf16[8,640,640]{2,1,0:T(8,128)(2,1)}, bf16[4,640,640]{2,1,0:T(8,128)(2,1)}, bf16[4,640,640]{2,1,0:T(8,128)(2,1)}) custom-call(s32[2,4]{1,0:T(2,128)} %bitcast.3, s32[4]{0:T(128)} %particles_ref.1, s32[4]{0:T(128)} %counts_ref.1, s32[32]{0:T(128)} %orbital_ref.1, f32[32,32]{1,0:T(8,128)} %integrals_ref.1, ...), custom_call_target="tpu_custom_call" | custom-call | tf_op jit(solution)/shard_map/pallas_call | solution.py:516
  303.0 15.8 %shard_map.114 = (bf16[8,640,640]{2,1,0:T(8,128)(2,1)}, bf16[8,640,640]{2,1,0:T(8,128)(2,1)}) custom-call(s32[2]{0:T(128)} %slice_reduce_fusion.ends_ref, bf16[8,640,640]{2,1,0:T(8,128)(2,1)} %get-tuple-element.6.normal_in, bf16[8,640,640]{2,1,0:T(8,128)(2,1)} %get-tuple-element.7.complementary_in, bf16[4,640,640]{2,1,0:T(8,128)(2,1)} %get-tuple-element.8.frame_in, ...), custom_call_target="tpu_custom_call" | custom-call | tf_op jit(solution)/shard_map/pallas_call | solution.py:573
